TPU v7x, 128 devices: a whole 4x4x4 slice. The times are simulated.
128 devices in a mesh: wide: 16 (over z, x_lo, core), tall: 8 (over x_hi, y).
Axes of the slice: x: 4 (x_hi: 2, x_lo: 2; x = x_hi * 2 + x_lo), y: 4, z: 4, core: 2. Of those that a mesh axis runs over, the one named last changes fastest.
Arguments:
- initial: float32 [16384, 16384], P(('wide', 'tall')), as said below
- child_tiles: float32 [8192, 128, 128], P(('wide', 'tall')), may hold values from -0.75 to 0.75
- child_targets: int32 [8192, 2], P(('wide', 'tall')), may hold values from 0 to 127, as said below
Outputs:
- front: float32 [16384, 16384], P('tall', 'wide')
Inputs may be any that keep to these rules, and one draw needn't show every extreme that they name: initial is symmetric, and assembled with its lower triangle mirrored is positive definite. `child_targets`: tile t * 8 + k of a device (t < 8, k < 8) lands on a block whose rows lie in the 128 rows of initial held by device g * 8 + t, g being the sender's index along wide; such a block's grid owner is the device at tall index (block row * 1) mod 8 and wide index (block column * 128 // 512) mod 16; the 8 tiles of one device with the same t go to 8 different grid owners, so one device sends at most one tile to one owner; in every grid row some owner gets one tile from every device.
All inputs are finite; a program needn't handle non-finite values.
Results may differ from a plain program's by a relative error of at most 0.0003.
Values sent between devices are 32-bit elements; how exact they have to be, the bound alone decides.
A program may use at most 192 MiB of HBM per device.

v0:
```python
import jax
import jax.numpy as jnp
import numpy as np
from jax import lax
from jax.sharding import PartitionSpec as P

PANEL = 512
PANELS = 2


full_precision = lax.Precision.HIGHEST


def from_root(value, axis, source):
    kept = jnp.where(lax.axis_index(axis) == source, value, 0).astype(value.dtype)
    return lax.psum(kept, axis)


def add_blocks(base, tiles, block_index, tile_edge):
    base_rows, base_cols = base.shape
    row_count = base_rows // tile_edge
    col_count = base_cols // tile_edge
    slot_ids = jnp.arange(row_count * col_count, dtype=jnp.int32)
    selector = (slot_ids[:, None] == block_index[None, :]).astype(jnp.float32)
    summed = jnp.dot(selector, tiles, precision=full_precision, preferred_element_type=jnp.float32)
    summed = summed.reshape(row_count, col_count, tile_edge, tile_edge).transpose(0, 2, 1, 3)
    return base + summed.reshape(base_rows, base_cols)


def relayout(slab, wide_size, panel_width):
    slab_rows, front_order = slab.shape
    col_tiles = front_order // (panel_width * wide_size)
    pieces_out = slab.reshape(slab_rows, col_tiles, wide_size, panel_width)
    arrived = lax.all_to_all(pieces_out, "wide", split_axis=2, concat_axis=0, tiled=True)
    return arrived.reshape(wide_size * slab_rows, col_tiles * panel_width)


def share_strip(front_local, panel_at, panel_width):
    wide_size = lax.axis_size("wide")
    home_tile = panel_at // wide_size
    column_piece = lax.slice_in_dim(
        front_local, home_tile * panel_width, (home_tile + 1) * panel_width, axis=1
    )
    return from_root(column_piece, "wide", panel_at % wide_size)


def block_tables(wanted, tall_size):
    owners = wanted % tall_size
    slots_at = wanted // tall_size
    width_wanted = wanted.shape[1]
    same_owner = owners[:, :, None] == owners[:, None, :]
    earlier = np.tril(np.ones((width_wanted, width_wanted), dtype=np.int32), -1)[None, :, :] > 0
    ranks = np.sum(same_owner & earlier, axis=2)
    piece_depth = int(np.max(ranks)) + 1
    talls = np.arange(tall_size)
    places = np.arange(piece_depth)
    matches = (owners[:, None, None, :] == talls[None, :, None, None]) & (
        ranks[:, None, None, :] == places[None, None, :, None]
    )
    senders = np.sum(matches * slots_at[:, None, None, :], axis=3).astype(np.int32)
    receivers = (owners * piece_depth + ranks).astype(np.int32)
    return (senders, receivers)


def owned_piece(source, senders, group_at, tall_at, slab_rows):
    slot_count = source.shape[0] // slab_rows
    blocks = source.reshape(slot_count, slab_rows, source.shape[1])
    chosen = jnp.asarray(senders)[group_at, tall_at]
    return jnp.take(blocks, chosen, axis=0)


def order_rows(gathered, receivers, group_at):
    placed = jnp.take(gathered, jnp.asarray(receivers)[group_at], axis=0)
    return placed.reshape(placed.shape[0] * placed.shape[1], placed.shape[2])


def body(initial, child_tiles, child_targets):
    wide_size = lax.axis_size("wide")
    tall_size = lax.axis_size("tall")
    wide_at = lax.axis_index("wide")
    tall_at = lax.axis_index("tall")
    slab_rows, front_order = initial.shape
    tile_count, tile_edge, _ = child_tiles.shape
    per_row = tile_count // tall_size
    panel_width = PANEL
    col_tiles = front_order // (panel_width * wide_size)
    blocks_per_panel = panel_width // slab_rows
    flat_tiles = child_tiles.reshape(tile_count, tile_edge * tile_edge)
    front_local = relayout(initial, wide_size, panel_width)
    target_wide = child_targets[:, 1] * tile_edge // panel_width % wide_size
    target_tall = jnp.arange(tile_count, dtype=jnp.int32) // per_row
    target_slot = target_wide * tall_size + target_tall
    slot_ids = jnp.arange(wide_size * tall_size, dtype=jnp.int32)
    selector = slot_ids[:, None] == target_slot[None, :]
    buffer = jnp.dot(
        selector.astype(jnp.float32),
        flat_tiles,
        precision=full_precision,
        preferred_element_type=jnp.float32,
    )
    filled = jnp.any(selector, axis=1)
    placed = jnp.sum(selector.astype(jnp.int32)[:, :, None] * child_targets[None, :, :], axis=1)
    placed = jnp.where(filled[:, None], placed, -1)
    arrived, targets = (
        lax.all_to_all(buffer, ("wide", "tall"), split_axis=0, concat_axis=0, tiled=True),
        lax.all_to_all(placed, ("wide", "tall"), split_axis=0, concat_axis=0, tiled=True),
    )
    usable = targets[:, 0] >= 0
    row_global = targets[:, 0] * tile_edge
    row_group = row_global // slab_rows
    local_row = row_group // tall_size * slab_rows + row_global % slab_rows
    col_global = targets[:, 1] * tile_edge
    local_col = col_global // panel_width // wide_size * panel_width + col_global % panel_width
    grid_index = (
        local_row // tile_edge * (col_tiles * panel_width // tile_edge) + local_col // tile_edge
    )
    grid_index = jnp.where(usable, grid_index, -1)
    front_local = add_blocks(front_local, arrived, grid_index, tile_edge)
    local_index = jnp.arange(front_local.shape[0], dtype=jnp.int32)
    global_row = (
        local_index // slab_rows * tall_size + tall_at
    ) * slab_rows + local_index % slab_rows
    tile_steps = np.arange(col_tiles)
    inner_steps = np.arange(blocks_per_panel)
    wide_steps = np.arange(wide_size)
    solved_wanted = (
        (tile_steps[None, :, None] * wide_size + wide_steps[:, None, None]) * blocks_per_panel
        + inner_steps[None, None, :]
    ).reshape(wide_size, col_tiles * blocks_per_panel)
    solved_send, solved_receive = block_tables(solved_wanted, tall_size)
    identity = jnp.eye(panel_width, dtype=jnp.float32)
    column_strip = share_strip(front_local, 0, panel_width)
    for panel_at in range(PANELS):
        low_row = panel_at * panel_width
        high_row = low_row + panel_width
        diag_wanted = (np.arange(blocks_per_panel) + low_row // slab_rows)[None, :]
        diag_send, diag_receive = block_tables(diag_wanted, tall_size)
        diag_piece = owned_piece(column_strip, diag_send, 0, tall_at, slab_rows)
        diag_block = order_rows(
            lax.all_gather(diag_piece, "tall", axis=0, tiled=True), diag_receive, 0
        )
        factor = jnp.linalg.cholesky(jnp.tril(diag_block) + jnp.tril(diag_block, -1).T)
        inverse = lax.linalg.triangular_solve(factor, identity, left_side=True, lower=True)
        solved = jnp.dot(
            column_strip, inverse.T, precision=full_precision, preferred_element_type=jnp.float32
        )
        below_mask = (global_row >= high_row)[:, None]
        inside = ((global_row >= low_row) & (global_row < high_row))[:, None]
        lower_rows = jnp.where(below_mask, solved, 0.0)
        new_diag = jnp.tril(factor) + jnp.triu(diag_block, 1)
        diag_rows = jnp.take(new_diag, jnp.clip(global_row - low_row, 0, panel_width - 1), axis=0)
        new_strip = jnp.where(below_mask, solved, jnp.where(inside, diag_rows, column_strip))
        solved_piece = owned_piece(lower_rows, solved_send, wide_at, tall_at, slab_rows)
        column_rows = order_rows(
            lax.all_gather(solved_piece, "tall", axis=0, tiled=True), solved_receive, wide_at
        )
        root_wide = panel_at % wide_size
        home_tile = panel_at // wide_size
        has_next = panel_at + 1 < PANELS
        change = jnp.dot(
            lower_rows, column_rows.T, precision=full_precision, preferred_element_type=jnp.float32
        )
        front_local = front_local - change
        current = lax.slice_in_dim(
            front_local, home_tile * panel_width, (home_tile + 1) * panel_width, axis=1
        )
        front_local = front_local.at[
            :, home_tile * panel_width : (home_tile + 1) * panel_width
        ].set(jnp.where(wide_at == root_wide, new_strip, current))
        if has_next:
            column_strip = share_strip(front_local, panel_at + 1, panel_width)
    return front_local


def solution(mesh):
    return jax.shard_map(
        body,
        mesh=mesh,
        in_specs=(
            P(("wide", "tall"), None),
            P(("wide", "tall"), None, None),
            P(("wide", "tall"), None),
        ),
        out_specs=P("tall", "wide"),
        check_vma=False,
    )
```

profile of v0, /device:TPU:1, one launch (start us, length us, event | category | flops | bytes accessed | tf_op | source)
XLA Modules:
  0.0 1217.7 jit_solution(8326474147539438546)
XLA Ops:
  8.9 11.5 all-to-all-start.1
  20.4 9.9 copy.62
  30.2 9.5 copy.39
  39.7 6.7 all-to-all-start
  46.5 8.4 convolution_bitcast_fusion
  54.8 9.8 copy.41
  64.6 76.3 %all-to-all-done = f32[128,2,16,512]{3,1,0,2:T(2,128)} async-done(((f32[128,2,16,512]{3,1,0,2:T(2,128)}), f32[128,2,16,512]{3,1,0,2:T(2,128)}, u32[]{:S(2)}, u32[]{:S(2)}) %all-to-all-start) | async-done | bytes 8388640 | tf_op jit(solution)/shard_map/all_to_all | solution.py:34
  140.9 8.4 all-to-all-start.2
  149.7 8.9 copy.63
  158.6 90.6 %all-to-all-done.2 = f32[128,1,16384]{2,1,0:T(1,128)} async-done(((f32[128,1,16384]{2,1,0:T(1,128)}), f32[128,1,16384]{2,1,0:T(1,128)}, u32[]{:S(2)}, u32[]{:S(2)}) %all-to-all-start.2) | async-done | bytes 8388640 | tf_op jit(solution)/shard_map/all_to_all | solution.py:105
  249.2 18.0 %copy.61 = f32[128,1,16384]{0,2,1:T(8,128)} copy(f32[128,1,16384]{2,1,0:T(1,128)} %all-to-all-done.2) | data formatting | bytes 16777216 | tf_op jit(solution)/shard_map/dot_general | solution.py:25
  267.2 11.2 fusion.82
  278.4 12.3 %bitcast_add_fusion = f32[2048,1024]{1,0:T(8,128)} fusion(f32[2048,1024]{1,0:T(8,128)} %bitcast.181, f32[256,8,8,128]{3,2,1,0:T(8,128)} %bitcast.182), kind=kLoop, calls=%fused_computation.13 | loop fusion | flops 2097152 | bytes 25165824 | tf_op jit(solution)/shard_map/add | solution.py:27
  290.7 4.7 slice_select_fusion
  295.4 135.7 %all-reduce.4.cloned.1.call-done = f32[2048,512]{1,0:T(8,128)} async-done(((f32[2048,512]{1,0:T(8,128)}), f32[2048,512]{1,0:T(8,128)}) %all-reduce.4.cloned.1.call-update) | async-done | bytes 4194320 | tf_op jit(solution)/shard_map/psum | solution.py:16
  435.1 52.9 %all-gather.5.cloned.1.call-done = f32[8,128,512]{2,1,0:T(8,128)} async-done(((f32[1,128,512]{2,1,0:T(8,128)}), f32[8,128,512]{2,1,0:T(8,128)}) %all-gather.5.cloned.1.call-update) | async-done | bytes 2097168 | tf_op jit(solution)/shard_map/all_gather | solution.py:140
  488.0 2.2 gather_fusion
  496.8 11.7 cholesky.286
  508.6 9.8 custom-call.27
  521.0 11.9 cholesky.305
  532.9 9.8 custom-call.28
  544.3 11.7 cholesky.326
  556.1 9.8 custom-call.29
  567.3 12.1 cholesky.343
  584.2 2.4 fusion.25
  586.6 11.6 while.7
  587.3 2.2 bitcast_dynamic-update-slice_fusion.4
  590.2 2.2 bitcast_dynamic-update-slice_fusion.4
  593.1 2.2 bitcast_dynamic-update-slice_fusion.4
  596.0 2.2 bitcast_dynamic-update-slice_fusion.4
  598.2 39.3 %custom-call.30 = f32[4,128,128]{1,2,0:T(8,128)S(1)} custom-call(f32[4,128,128]{2,1,0:T(8,128)S(1)} %get-tuple-element.61), custom_call_target="InvertDiagBlocksLowerTriangular" | custom-call | tf_op jit(solution)/shard_map/triangular_solve/custom-call.3 | solution.py:143
  643.6 9.0 broadcast_select_fusion.2
  652.6 2.8 gather_fusion.1
  657.3 8.9 gather_fusion.3
  666.2 59.4 %all-gather.7.cloned.1.call-done = f32[16,128,512]{2,1,0:T(8,128)} async-done(((f32[2,128,512]{2,1,0:T(8,128)}), f32[16,128,512]{2,1,0:T(8,128)}) %all-gather.7.cloned.1.call-update) | async-done | bytes 4194320 | tf_op jit(solution)/shard_map/all_gather | solution.py:155
  725.6 2.9 gather_fusion.2
  730.7 17.0 %convolution_subtract_fusion.1 = f32[2048,1024]{1,0:T(8,128)S(1)} fusion(f32[2048,1024]{1,0:T(8,128)} %bitcast_add_fusion, f32[2048,512]{1,0:T(8,128)S(1)} %copy-done.1, f32[1024,512]{1,0:T(8,128)S(1)} %bitcast.191), kind=kOutput, calls=%fused_computation.25 | convolution fusion | flops 12886999040 | bytes 23068672 | tf_op jit(solution)/shard_map/dot_general | solution.py:160
  747.7 6.1 broadcast_select_fusion.1
  753.9 133.2 %all-reduce.6.cloned.1.call-done = f32[2048,512]{1,0:T(8,128)} async-done(((f32[2048,512]{1,0:T(8,128)}), f32[2048,512]{1,0:T(8,128)}) %all-reduce.6.cloned.1.call-update) | async-done | bytes 4194320 | tf_op jit(solution)/shard_map/psum | solution.py:16
  889.1 54.7 %all-gather.9.cloned.1.call-done = f32[8,128,512]{2,1,0:T(8,128)} async-done(((f32[1,128,512]{2,1,0:T(8,128)}), f32[8,128,512]{2,1,0:T(8,128)}) %all-gather.9.cloned.1.call-update) | async-done | bytes 2097168 | tf_op jit(solution)/shard_map/all_gather | solution.py:140
  943.9 2.2 gather_fusion.4
  953.0 11.7 cholesky.358
  964.8 9.8 custom-call.31
  977.2 11.7 cholesky.377
  988.9 10.2 custom-call.32
  1000.7 11.7 cholesky.398
  1012.4 9.8 custom-call.33
  1023.7 11.9 cholesky.415
  1040.7 2.5 fusion.22
  1043.2 10.8 while.8
  1043.8 2.1 bitcast_dynamic-update-slice_fusion.5
  1046.5 2.1 bitcast_dynamic-update-slice_fusion.5
  1049.2 2.1 bitcast_dynamic-update-slice_fusion.5
  1051.9 2.0 bitcast_dynamic-update-slice_fusion.5
  1054.0 39.3 %custom-call.34 = f32[4,128,128]{1,2,0:T(8,128)S(1)} custom-call(f32[4,128,128]{2,1,0:T(8,128)S(1)} %get-tuple-element.62), custom_call_target="InvertDiagBlocksLowerTriangular" | custom-call | tf_op jit(solution)/shard_map/triangular_solve/custom-call.3 | solution.py:143
  1099.4 8.9 broadcast_select_fusion
  1108.3 2.8 gather_fusion.5
  1112.1 4.6 constant_dynamic-update-slice_fusion.6
  1116.7 8.9 gather_fusion.7
  1125.6 55.7 %all-gather.11.cloned.1.call-done = f32[16,128,512]{2,1,0:T(8,128)} async-done(((f32[2,128,512]{2,1,0:T(8,128)}), f32[16,128,512]{2,1,0:T(8,128)}) %all-gather.11.cloned.1.call-update) | async-done | bytes 4194320 | tf_op jit(solution)/shard_map/all_gather | solution.py:155
  1181.4 2.9 gather_fusion.6
  1184.6 1.9 copy-done.2
  1186.4 17.8 %convolution_subtract_fusion = f32[2048,1024]{1,0:T(8,128)} fusion(f32[2048,1024]{1,0:T(8,128)} %constant_dynamic-update-slice_fusion.6, f32[2048,512]{1,0:T(8,128)S(1)} %copy-done.2, f32[1024,512]{1,0:T(8,128)S(1)} %bitcast.190), kind=kOutput, calls=%fused_computation.24 | convolution fusion | flops 12886999040 | bytes 23068672 | tf_op jit(solution)/shard_map/dot_general | solution.py:160
  1204.3 6.4 fusion
  (154 shorter events, 60.9 us)
Async XLA Ops:
  8.9 30.9 %all-to-all-start.1 = ((s32[128,1,2]{2,1,0:T(1,128)}), s32[128,1,2]{2,1,0:T(1,128)S(1)}, u32[]{:S(2)}, u32[]{:S(2)}) async-start(s32[128,1,2]{2,1,0:T(1,128)} %copy.40), calls=%async_computation.1 | async-start | bytes 131072 | tf_op jit(solution)/shard_map/all_to_all | solution.py:106
  39.7 101.2 %all-to-all-start = ((f32[128,2,16,512]{3,1,0,2:T(2,128)}), f32[128,2,16,512]{3,1,0,2:T(2,128)}, u32[]{:S(2)}, u32[]{:S(2)}) async-start(f32[128,2,16,512]{3,1,0,2:T(2,128)} %copy.39), calls=%async_computation | async-start | bytes 16777216 | tf_op jit(solution)/shard_map/all_to_all | solution.py:34
  140.9 108.2 %all-to-all-start.2 = ((f32[128,1,16384]{2,1,0:T(1,128)}), f32[128,1,16384]{2,1,0:T(1,128)}, u32[]{:S(2)}, u32[]{:S(2)}) async-start(f32[128,1,16384]{2,1,0:T(1,128)} %copy.41), calls=%async_computation.2 | async-start | bytes 16777216 | tf_op jit(solution)/shard_map/all_to_all | solution.py:105
  149.3 281.7 %all-reduce.4.cloned.1.call-start = ((), (), s32[]{:S(2)}) async-start(), calls=%async_computation.3 | async-start | bytes 8388608 | tf_op jit(solution)/shard_map/psum | solution.py:16
  295.3 192.6 %all-gather.5.cloned.1.call-start = ((), (), s32[]{:S(2)}) async-start(), calls=%async_computation.4 | async-start | bytes 2359296 | tf_op jit(solution)/shard_map/all_gather | solution.py:140
  432.8 292.9 %all-gather.7.cloned.1.call-start = ((), (), s32[]{:S(2)}) async-start(), calls=%async_computation.5 | async-start | bytes 4718592 | tf_op jit(solution)/shard_map/all_gather | solution.py:155
  495.8 1.0 copy-start.13
  579.5 4.7 copy-start.11
  637.5 6.1 copy-start.3
  656.3 230.8 %all-reduce.6.cloned.1.call-start = ((), (), s32[]{:S(2)}) async-start(), calls=%async_computation.6 | async-start | bytes 8388608 | tf_op jit(solution)/shard_map/psum | solution.py:16
  728.5 2.2 copy-start.1
  730.7 17.0 %copy-start.4 = (f32[2048,512]{1,0:T(8,128)S(1)}, f32[2048,512]{1,0:T(8,128)}, u32[]{:S(2)}) copy-start(f32[2048,512]{1,0:T(8,128)} %all-reduce.4.cloned.1.call-done) | copy-start | bytes 12582916
  730.7 17.0 %copy-start.7 = (f32[2048,512]{1,0:T(8,128)S(1)}, f32[2048,512]{1,0:T(8,128)}, u32[]{:S(2)}) copy-start(f32[2048,512]{1,0:T(8,128)} %gather_fusion.3) | copy-start | bytes 12582916
  730.7 17.1 %copy-start.8 = (f32[2048,512]{1,0:T(8,128)S(1)}, f32[2048,512]{1,0:T(8,128)}, u32[]{:S(2)}) copy-start(f32[2048,512]{1,0:T(8,128)} %get-tuple-element.120) | copy-start | bytes 12582916
  747.7 6.1 copy-start
  753.8 135.3 %copy-start.15 = (s32[4]{0:T(128)S(1)}, s32[4]{0:T(128)}, u32[]{:S(2)}) copy-start(s32[4]{0:T(128)} %constant.489) | copy-start | bytes 52
  753.9 190.0 %all-gather.9.cloned.1.call-start = ((), (), s32[]{:S(2)}) async-start(), calls=%async_computation.7 | async-start | bytes 2359296 | tf_op jit(solution)/shard_map/all_gather | solution.py:140
  888.8 292.5 %all-gather.11.cloned.1.call-start = ((), (), s32[]{:S(2)}) async-start(), calls=%async_computation.8 | async-start | bytes 4718592 | tf_op jit(solution)/shard_map/all_gather | solution.py:155
  951.9 1.1 copy-start.14
  1035.6 5.1 copy-start.12
  1093.3 6.1 copy-start.5
  1184.2 2.2 copy-start.2
  1186.4 17.8 %copy-start.6 = (f32[2048,512]{1,0:T(8,128)S(1)}, f32[2048,512]{1,0:T(8,128)}, u32[]{:S(2)}) copy-start(f32[2048,512]{1,0:T(8,128)} %all-reduce.6.cloned.1.call-done) | copy-start | bytes 12582916
  1186.4 17.8 %copy-start.9 = (f32[2048,512]{1,0:T(8,128)S(1)}, f32[2048,512]{1,0:T(8,128)}, u32[]{:S(2)}) copy-start(f32[2048,512]{1,0:T(8,128)} %gather_fusion.7) | copy-start | bytes 12582916
  1186.4 17.8 %copy-start.10 = (f32[2048,512]{1,0:T(8,128)S(1)}, f32[2048,512]{1,0:T(8,128)}, u32[]{:S(2)}) copy-start(f32[2048,512]{1,0:T(8,128)} %get-tuple-element.124) | copy-start | bytes 12582916
Sparse Core Ops, SparseCore 0:
  295.4 135.5 all-reduce.3
  433.4 54.5 all-gather.4
  656.4 69.1 all-gather.6
  754.0 133.0 all-reduce.5
  889.3 54.5 all-gather.8
  1112.2 69.1 all-gather.10
where the time goes:
time: 1230 us; the launch traced here: 1220 us
  waiting for transfers between devices  659 us (54%)
  other arithmetic  285 us (23%)
  local copies, waits for them, and re-layouts  132 us (11%)
  matrix products  95.2 us (8%)
  starting transfers between devices  27.4 us (2%)
  between operations  19.3 us (2%)
    psum x2, waiting for transfers between devices, from_root(): return lax.psum(kept, axis)  269 us
    another operation x29, other arithmetic, body(): jnp.linalg.cholesky(jnp.tril(diag_block) + jnp.tril(diag_block, -1).T)  159 us
    all_gather x2, waiting for transfers between devices, body(): lax.all_gather(solved_piece, 'tall', axis=0, tiled=True)  115 us
    all_gather x2, waiting for transfers between devices, body(): lax.all_gather(diag_piece, 'tall', axis=0, tiled=True)  108 us
    all_to_all x1, waiting for transfers between devices, body(): lax.all_to_all(buffer, ('wide', 'tall'), split_axis=0, concat_axis=0, til...  90.6 us
    another operation x4, other arithmetic, body(): lax.linalg.triangular_solve(factor, identity, left_side=True, lower=True)  78.7 us
    all_to_all x1, waiting for transfers between devices, relayout(): lax.all_to_all(pieces_out, 'wide', split_axis=2, concat_axis=0, tiled=True)  76.3 us
    dot_general x2, matrix products, body(): jnp.dot(lower_rows, column_rows.T, precision=full_precision, preferred_el...  34.8 us
  transfers between devices with their start and end apart: 9, of which 8 were waited for; matrix products, arithmetic and copies ran while one was open for 6% of the time, Pallas kernels for 0%

commit v1 on v0

v1 whole, which is shorter than its diff:
```python
import functools

import jax
import jax.numpy as jnp
from jax import lax
from jax.experimental import pallas as pl
from jax.experimental.pallas import tpu as pltpu
from jax.sharding import PartitionSpec as P

PANEL = 512
LEAD = 1024
B = 128
MESH = pl.DeviceIdType.MESH
NT = (((1,), (1,)), ((), ()))
NN = (((1,), (0,)), ((), ()))
VMEM_LIMIT = 60 * 1024 * 1024
F32 = jnp.float32


def vmem_spec():
    return pl.BlockSpec(memory_space=pltpu.VMEM)


def any_spec():
    return pl.BlockSpec(memory_space=pl.ANY)


def params(**more):
    return pltpu.CompilerParams(vmem_limit_bytes=VMEM_LIMIT, **more)


def add_kernel(cols_ref, initial_ref, tiles_ref, out_ref, strip_ref, acc, tiles, sem_in, sem_tile, sem_out, sem_strip):
    wides = acc.shape[0]
    halves = acc.shape[2] // PANEL
    count = tiles.shape[0]
    loads = []
    for q in range(halves):
        for w in range(wides):
            at = (q * wides + w) * PANEL
            loads.append(
                pltpu.make_async_copy(
                    initial_ref.at[:, at : at + PANEL],
                    acc.at[w, :, q * PANEL : (q + 1) * PANEL],
                    sem_in.at[q * wides + w],
                )
            )
    tile_load = pltpu.make_async_copy(tiles_ref, tiles, sem_tile)
    for load in loads:
        load.start()
    tile_load.start()
    for load in loads:
        load.wait()
    tile_load.wait()
    per_panel = PANEL // B

    def add(n, carry):
        col = cols_ref[n]
        block = col // per_panel
        at = pl.multiple_of((block // wides) * PANEL + (col % per_panel) * B, B)
        acc[block % wides, :, pl.ds(at, B)] += tiles[n]
        return carry

    lax.fori_loop(0, count, add, 0)
    stores = [
        pltpu.make_async_copy(acc.at[0, :, 0:PANEL], strip_ref.at[:, 0:PANEL], sem_strip.at[0]),
        pltpu.make_async_copy(acc.at[1, :, 0:PANEL], strip_ref.at[:, PANEL:LEAD], sem_strip.at[1]),
    ]
    for w in range(wides):
        stores.append(pltpu.make_async_copy(acc.at[w], out_ref.at[w], sem_out.at[w]))
    for store in stores:
        store.start()
    for store in stores:
        store.wait()


def add_tiles(initial, tiles, cols, wides):
    rows, order = initial.shape
    count = tiles.shape[0]
    width = order // wides
    return pl.pallas_call(
        add_kernel,
        grid_spec=pltpu.PrefetchScalarGridSpec(
            num_scalar_prefetch=1,
            grid=(1,),
            in_specs=[any_spec(), any_spec()],
            out_specs=[any_spec(), any_spec()],
            scratch_shapes=[
                pltpu.VMEM((wides, rows, width), F32),
                pltpu.VMEM((count, B, B), F32),
                pltpu.SemaphoreType.DMA((order // PANEL,)),
                pltpu.SemaphoreType.DMA,
                pltpu.SemaphoreType.DMA((wides,)),
                pltpu.SemaphoreType.DMA((2,)),
            ],
        ),
        out_shape=[
            jax.ShapeDtypeStruct((wides, rows, width), F32),
            jax.ShapeDtypeStruct((rows, LEAD), F32),
        ],
        compiler_params=params(),
        name="add_tiles",
    )(cols, initial, tiles)


def place():
    w = lax.axis_index("wide")
    t = lax.axis_index("tall")
    z, x, c = w // 4, (w // 2) % 2, w % 2
    h, y = t // 4, t % 4
    return w, t, z, x, c, h, y


def wide_at(z, x, c):
    return lax.rem(z + 4, 4) * 4 + x * 2 + c


def tall_at(h, y):
    return h * 4 + lax.rem(y + 4, 4)


def neighbours():
    w, t, z, x, c, h, y = place()
    return {
        "up": (wide_at(z + 1, x, c), t),
        "down": (wide_at(z - 1, x, c), t),
        "side": (wide_at(z, 1 - x, c), t),
        "core": (wide_at(z, x, 1 - c), t),
        "far": (w, tall_at(1 - h, y)),
        "north": (w, tall_at(h, y + 1)),
        "south": (w, tall_at(h, y - 1)),
    }


def greet(partners):
    barrier = pltpu.get_barrier_semaphore()
    for partner in partners:
        pl.semaphore_signal(barrier, inc=1, device_id=partner, device_id_type=MESH)
    pl.semaphore_wait(barrier, len(partners))


def send(src, dst, send_sem, recv_sem, partner):
    copy = pltpu.make_async_remote_copy(
        src_ref=src, dst_ref=dst, send_sem=send_sem, recv_sem=recv_sem,
        device_id=partner, device_id_type=MESH,
    )
    copy.start()
    return copy


def arrived(ref, sem):
    pltpu.make_async_copy(ref, ref, sem).wait()


CHUNKS = 4


def lead_kernel(strip_ref, lead_ref, send_sem, recv_sem, core_sem, local_sem):
    w, t, z, x, c, h, y = place()
    side = neighbours()
    greet(list(side.values()))
    half = B // 2
    rows = half // CHUNKS
    sent = []

    def piece(block, core, n):
        return lead_ref.at[block, pl.ds(core * half + n * rows, rows), :]

    def push(block, core, n, to, sem, slot):
        copy = pltpu.make_async_remote_copy(
            src_ref=piece(block, core, n), dst_ref=piece(block, core, n),
            send_sem=send_sem.at[slot, n], recv_sem=sem.at[block, n],
            device_id=side[to], device_id_type=MESH,
        )
        return copy

    def go(pred, copy):
        if pred is None:
            copy.start()
            sent.append((None, copy))
        else:
            @pl.when(pred)
            def _():
                copy.start()
            sent.append((pred, copy))

    other = 1 - c
    far = tall_at(1 - h, y)
    is_root = w == 0
    own = pltpu.make_async_copy(strip_ref, lead_ref.at[t], local_sem)

    @pl.when(is_root)
    def _():
        own.start()
        own.wait()

    for n in range(CHUNKS):
        go(is_root, push(t, 1, n, "core", recv_sem, 0))
    for n in range(CHUNKS):
        @pl.when(w != 0)
        def _():
            arrived(piece(t, c, n), recv_sem.at[t, n])
        base = x == 0
        go(base & (z == 0), push(t, c, n, "up", recv_sem, 1))
        go(base & (z == 0), push(t, c, n, "down", recv_sem, 2))
        if n % 2 == 0:
            go(base & (z == 1), push(t, c, n, "up", recv_sem, 1))
        else:
            go(base & (z == 3), push(t, c, n, "down", recv_sem, 2))
        go(base, push(t, c, n, "side", recv_sem, 3))
        go(None, push(t, c, n, "far", recv_sem, 4))
        go(None, push(t, c, n, "north", recv_sem, 5))
        go(None, push(t, c, n, "south", recv_sem, 6))
        go(w > 1, push(t, c, n, "core", core_sem, 0))
        go(w == 0, push(t, c, n, "core", core_sem, 7))
    for n in range(CHUNKS):
        arrived(piece(far, c, n), recv_sem.at[far, n])
        go(None, push(far, c, n, "north", recv_sem, 8))
        go(None, push(far, c, n, "south", recv_sem, 9))
        go(None, push(far, c, n, "core", core_sem, 10))
    for n in range(CHUNKS):
        slot = 11
        for hh in (h, 1 - h):
            for step, to in ((-1, "north"), (1, "south")):
                block = tall_at(hh, y + step)
                arrived(piece(block, c, n), recv_sem.at[block, n])
                if n % 2 == (0 if to == "north" else 1):
                    go(None, push(block, c, n, to, recv_sem, slot))
                go(None, push(block, c, n, "core", core_sem, slot + 1))
                slot += 2
    for n in range(CHUNKS):
        for i, hh in enumerate((h, 1 - h)):
            block = tall_at(hh, y + 2)
            arrived(piece(block, c, n), recv_sem.at[block, n])
            go(None, push(block, c, n, "core", core_sem, 19 + i))
    for n in range(CHUNKS):
        for block in range(8):
            @pl.when((w != 0) | (block != t))
            def _():
                arrived(piece(block, other, n), core_sem.at[block, n])
    for pred, copy in sent:
        if pred is None:
            copy.wait_send()
        else:
            @pl.when(pred)
            def _():
                copy.wait_send()


def share_lead(strip):
    return pl.pallas_call(
        lead_kernel,
        out_shape=jax.ShapeDtypeStruct((LEAD // B, B, LEAD), F32),
        in_specs=[vmem_spec()],
        out_specs=vmem_spec(),
        scratch_shapes=[
            pltpu.SemaphoreType.DMA((21, CHUNKS)),
            pltpu.SemaphoreType.DMA((8, CHUNKS)),
            pltpu.SemaphoreType.DMA((8, CHUNKS)),
            pltpu.SemaphoreType.DMA,
        ],
        compiler_params=params(collective_id=0, has_side_effects=True),
        name="share_lead",
    )(strip)


def lane(x, c):
    return jnp.broadcast_to(x[:, c : c + 1], (x.shape[0], B))


def row(x, r):
    return jnp.broadcast_to(x[r : r + 1, :], (8, x.shape[1]))


def factor_block(dref, vref):
    for m in range(B // 8):
        c0 = 8 * m
        p = dref[c0 : c0 + 8, :]
        wp = vref[c0 : c0 + 8, :]
        q = [lane(p, c0 + k) for k in range(8)]
        s = [[row(q[j], i) if j <= i else None for j in range(8)] for i in range(8)]
        f = [[None] * 8 for _ in range(8)]
        dinv = [None] * 8
        for j in range(8):
            dinv[j] = 1.0 / s[j][j]
            for i in range(j + 1, 8):
                f[i][j] = s[i][j] * dinv[j]
            for i in range(j + 1, 8):
                for k in range(j + 1, i + 1):
                    s[i][k] = s[i][k] - f[i][j] * s[k][j]
        r = [row(p, j) for j in range(8)]
        rw = [row(wp, j) for j in range(8)]
        for j in range(8):
            for i in range(j + 1, 8):
                r[i] = r[i] - f[i][j] * r[j]
                rw[i] = rw[i] - f[i][j] * rw[j]
        u = [r[j] * dinv[j] for j in range(8)]
        uw = [rw[j] * dinv[j] for j in range(8)]
        for j in range(7, 0, -1):
            for i in range(j):
                u[i] = u[i] - f[j][i] * u[j]
                uw[i] = uw[i] - f[j][i] * uw[j]
        for v in range(m + 1, B // 8):
            rows = dref[8 * v : 8 * v + 8, :]
            wrows = vref[8 * v : 8 * v + 8, :]
            acc = accw = None
            for j in range(8):
                c = lane(rows, c0 + j)
                acc = c * u[j] if acc is None else acc + c * u[j]
                accw = c * uw[j] if accw is None else accw + c * uw[j]
            dref[8 * v : 8 * v + 8, :] = rows - acc
            vref[8 * v : 8 * v + 8, :] = wrows - accw
        sub = lax.broadcasted_iota(jnp.int32, (8, B), 0)
        out = outw = None
        for j in range(8):
            scale = lax.rsqrt(s[j][j])
            a, b = r[j] * scale, rw[j] * scale
            out = a if out is None else jnp.where(sub == j, a, out)
            outw = b if outw is None else jnp.where(sub == j, b, outw)
        dref[c0 : c0 + 8, :] = out
        vref[c0 : c0 + 8, :] = outw


def split(x):
    high = x.astype(jnp.bfloat16)
    low = (x - high.astype(F32)).astype(jnp.bfloat16)
    return high, low


def dot3(a, b, dims):
    d = functools.partial(lax.dot_general, dimension_numbers=dims, preferred_element_type=F32)
    return d(a[0], b[0]) + (d(a[0], b[1]) + d(a[1], b[0]))


def dot6(a, b, dims):
    return lax.dot_general(a, b, dims, precision=lax.Precision.HIGHEST, preferred_element_type=F32)


def factor_lead(a, w, dblk, vblk, lcol):
    n = a.shape[0]
    blocks = n // B
    ri = lax.broadcasted_iota(jnp.int32, (B, B), 0)
    ci = lax.broadcasted_iota(jnp.int32, (B, B), 1)
    eye = jnp.where(ri == ci, 1.0, 0.0).astype(F32)
    wi = lax.broadcasted_iota(jnp.int32, (B, n), 0)
    wj = lax.broadcasted_iota(jnp.int32, (B, n), 1)
    for i in range(blocks):
        w[i * B : (i + 1) * B, :] = jnp.where(wi + i * B == wj, 1.0, 0.0)

    def step(j, carry):
        o = pl.multiple_of(j * B, B)
        d = a[pl.ds(o, B), pl.ds(o, B)]
        dblk[...] = jnp.where(ri >= ci, d, d.T)
        vblk[...] = eye
        factor_block(dblk, vblk)
        a[pl.ds(o, B), pl.ds(o, B)] = jnp.where(ri <= ci, dblk[...], 0.0).T
        winv = vblk[...]
        wrow = dot6(winv, w[pl.ds(o, B), :], NN)
        w[pl.ds(o, B), :] = wrow

        def solve(i, c):
            r = pl.multiple_of(i * B, B)
            solved = dot6(a[pl.ds(r, B), pl.ds(o, B)], winv, NT)
            a[pl.ds(r, B), pl.ds(o, B)] = solved
            lcol[pl.ds(r, B), :] = solved
            return c

        lax.fori_loop(j + 1, blocks, solve, 0)

        def update(i, c):
            r = pl.multiple_of(i * B, B)
            mine = lcol[pl.ds(r, B), :]
            w[pl.ds(r, B), :] -= dot6(mine, wrow, NN)

            def cols(k, cc):
                s = pl.multiple_of(k * B, B)
                a[pl.ds(r, B), pl.ds(s, B)] -= dot6(mine, lcol[pl.ds(s, B), :], NT)
                return cc

            lax.fori_loop(j + 1, i + 1, cols, 0)
            return c

        lax.fori_loop(j + 1, blocks, update, 0)
        return carry

    lax.fori_loop(0, blocks, step, 0)


def factor_kernel(lead_ref, strip_ref, solved_ref, shown_ref, a, w, dblk, vblk, lcol):
    wide = lax.axis_index("wide")
    tall = lax.axis_index("tall")
    a[...] = lead_ref[...]
    factor_lead(a, w, dblk, vblk, lcol)
    shown_ref[...] = a[pl.ds(pl.multiple_of(tall * B, B), B), :]
    solved = dot6(strip_ref[...], w[...], NT)
    cols = lax.broadcasted_iota(jnp.int32, solved.shape, 1)
    keep = (wide > 0) | ((tall >= PANEL // B) & (cols < PANEL))
    solved_ref[...] = jnp.where(keep, solved, 0.0)


def factor_and_solve(lead, strip):
    return pl.pallas_call(
        factor_kernel,
        out_shape=(jax.ShapeDtypeStruct((B, LEAD), F32),) * 2,
        in_specs=[vmem_spec()] * 2,
        out_specs=(vmem_spec(),) * 2,
        scratch_shapes=[
            pltpu.VMEM((LEAD, LEAD), F32),
            pltpu.VMEM((LEAD, LEAD), F32),
            pltpu.VMEM((B, B), F32),
            pltpu.VMEM((B, B), F32),
            pltpu.VMEM((LEAD, B), F32),
        ],
        compiler_params=params(),
        name="factor",
    )(lead, strip)


def share_kernel(mine_ref, rows_ref, cols_ref, hold, send_sem, row_sem, col_sem, local_sem):
    w, t, z, x, c, h, y = place()
    side = neighbours()
    half = B // 2
    target = 2 * lax.rem(w, 8) + h
    quarter = w // 8
    partners = list(side.values())
    greet(partners)
    sent = []
    count = [0]

    def push(ref, sem, to):
        slot = count[0]
        count[0] += 1
        return pltpu.make_async_remote_copy(
            src_ref=ref, dst_ref=ref, send_sem=send_sem.at[slot], recv_sem=sem,
            device_id=side[to], device_id_type=MESH,
        )

    def go(copy, pred=None):
        if pred is None:
            copy.start()
        else:
            @pl.when(pred)
            def _():
                copy.start()
        sent.append((pred, copy))

    def rpiece(k, n):
        return rows_ref.at[k, pl.ds(n * half, half), :]

    def cpiece(q, i, n):
        return cols_ref.at[q * 4 + i, pl.ds(n * half, half), :]

    own = pltpu.make_async_copy(mine_ref, rows_ref.at[w], local_sem.at[0])
    own.start()

    def first(n, to):
        slot = count[0]
        count[0] += 1
        return pltpu.make_async_remote_copy(
            src_ref=mine_ref.at[pl.ds(n * half, half), :], dst_ref=rpiece(w, n),
            send_sem=send_sem.at[slot], recv_sem=row_sem.at[w, n],
            device_id=side[to], device_id_type=MESH,
        )

    for n in range(2):
        for to in ("side", "up", "down", "core"):
            go(first(n, to))
    beside = wide_at(z, 1 - x, c)
    for n in range(2):
        arrived(rpiece(beside, n), row_sem.at[beside, n])
        for to in ("up", "down", "core"):
            go(push(rpiece(beside, n), row_sem.at[beside, n], to))
    for xx in (x, 1 - x):
        for n in range(2):
            for dz, to, part in ((-1, "up", 0), (1, "down", 1)):
                k = wide_at(z + dz, xx, c)
                arrived(rpiece(k, n), row_sem.at[k, n])
                if n == part:
                    go(push(rpiece(k, n), row_sem.at[k, n], to))
                go(push(rpiece(k, n), row_sem.at[k, n], "core"))
    for xx in (x, 1 - x):
        for n in range(2):
            k = wide_at(z + 2, xx, c)
            arrived(rpiece(k, n), row_sem.at[k, n])
            go(push(rpiece(k, n), row_sem.at[k, n], "core"))
    for zz in (z, z - 1, z + 1, z + 2):
        for xx in (x, 1 - x):
            k = wide_at(zz, xx, 1 - c)
            for n in range(2):
                arrived(rpiece(k, n), row_sem.at[k, n])
    own.wait()
    pair = w // 2
    holder = h == c
    for q in range(2):
        k = q * 8 + pair

        @pl.when(holder)
        def _():
            take = pltpu.make_async_copy(rows_ref.at[k], hold.at[q], local_sem.at[1])
            take.start()
            take.wait()
            put = pltpu.make_async_copy(hold.at[q], cols_ref.at[q * 4 + y], local_sem.at[1])
            put.start()
            put.wait()
    for q in range(2):
        for n in range(2):
            @pl.when(jnp.logical_not(holder))
            def _():
                arrived(cpiece(q, y, n), col_sem.at[q, y, n])
            go(push(cpiece(q, y, n), col_sem.at[q, y, n], "far"), holder)
            go(push(cpiece(q, y, n), col_sem.at[q, y, n], "north"))
            go(push(cpiece(q, y, n), col_sem.at[q, y, n], "south"))
    for q in range(2):
        for n in range(2):
            for dy, to, part in ((-1, "north", 0), (1, "south", 1)):
                i = lax.rem(y + dy + 4, 4)
                arrived(cpiece(q, i, n), col_sem.at[q, i, n])
                if n == part:
                    go(push(cpiece(q, i, n), col_sem.at[q, i, n], to))
    for q in range(2):
        for n in range(2):
            i = lax.rem(y + 2, 4)
            arrived(cpiece(q, i, n), col_sem.at[q, i, n])
    for pred, copy in sent:
        if pred is None:
            copy.wait_send()
        else:
            @pl.when(pred)
            def _():
                copy.wait_send()


def share_solved(mine):
    return pl.pallas_call(
        share_kernel,
        out_shape=(
            jax.ShapeDtypeStruct((16, B, LEAD), F32),
            jax.ShapeDtypeStruct((8, B, LEAD), F32),
        ),
        in_specs=[vmem_spec()],
        out_specs=(any_spec(), any_spec()),
        scratch_shapes=[
            pltpu.VMEM((2, B, LEAD), F32),
            pltpu.SemaphoreType.DMA((64,)),
            pltpu.SemaphoreType.DMA((16, 2)),
            pltpu.SemaphoreType.DMA((2, 4, 2)),
            pltpu.SemaphoreType.DMA((2,)),
        ],
        compiler_params=params(collective_id=1, has_side_effects=True),
        name="share_solved",
    )(mine)


def update_kernel(front_ref, rows_ref, cols_ref, shown_ref, out_ref, high, low):
    step = pl.program_id(0)
    wide = lax.axis_index("wide")
    tall = lax.axis_index("tall")

    @pl.when(step == 0)
    def _():
        for i in range(LEAD // B):
            h, l = split(cols_ref[i * B : (i + 1) * B, :])
            high[i * B : (i + 1) * B, :] = h
            low[i * B : (i + 1) * B, :] = l

    mine = rows_ref[...]
    change = dot3(split(mine), (high[...], low[...]), NT)
    out = front_ref[...] - change
    out_ref[...] = out
    for p in range(2):
        @pl.when(wide == p)
        def _():
            out_ref[:, 0:PANEL] = mine[:, p * PANEL : (p + 1) * PANEL]

            @pl.when(step == 0)
            def _():
                r = lax.broadcasted_iota(jnp.int32, (B, PANEL), 0) + tall * B
                c = lax.broadcasted_iota(jnp.int32, (B, PANEL), 1) + p * PANEL
                out_ref[0:B, 0:PANEL] = jnp.where(
                    r >= c, shown_ref[:, p * PANEL : (p + 1) * PANEL], out[0:B, 0:PANEL]
                )


def update(front, rows, cols, shown):
    total, width = front.shape
    chunk = 256
    return pl.pallas_call(
        update_kernel,
        grid=(total // chunk,),
        out_shape=jax.ShapeDtypeStruct(front.shape, F32),
        in_specs=[
            pl.BlockSpec((chunk, width), lambda i: (i, 0)),
            pl.BlockSpec((chunk, LEAD), lambda i: (i, 0)),
            pl.BlockSpec((width, LEAD), lambda i: (0, 0)),
            pl.BlockSpec((B, LEAD), lambda i: (0, 0)),
        ],
        out_specs=pl.BlockSpec((chunk, width), lambda i: (i, 0)),
        scratch_shapes=[pltpu.VMEM((width, LEAD), jnp.bfloat16)] * 2,
        compiler_params=params(),
        name="update",
    )(front, rows, cols, shown)


def body(initial, child_tiles, child_targets):
    wides = lax.axis_size("wide")
    cols = lax.all_to_all(child_targets[:, 1], "tall", split_axis=0, concat_axis=0, tiled=True)
    tiles = lax.all_to_all(child_tiles, "tall", split_axis=0, concat_axis=0, tiled=True)
    slab, strip = add_tiles(initial, tiles, cols, wides)
    lead = share_lead(strip)
    slab, lead = lax.optimization_barrier((slab, lead))
    front = lax.all_to_all(slab, "wide", split_axis=0, concat_axis=0, tiled=True)
    solved, shown = factor_and_solve(lead.reshape(LEAD, LEAD), strip)
    rows, columns = share_solved(solved)
    front = front.reshape(-1, slab.shape[2])
    return update(front, rows.reshape(-1, LEAD), columns.reshape(-1, LEAD), shown)


def solution(mesh):
    return jax.shard_map(
        body,
        mesh=mesh,
        in_specs=(
            P(("wide", "tall"), None),
            P(("wide", "tall"), None, None),
            P(("wide", "tall"), None),
        ),
        out_specs=P("tall", "wide"),
        check_vma=False,
    )
```

time: 1230 us -> 332 us (0.27)
  waiting for transfers between devices: 659 us -> 46.8 us
  other arithmetic: 285 us -> 0.66 us
  Pallas kernels: 0 us -> 249 us
  local copies, waits for them, and re-layouts: 132 us -> 1.96 us
  matrix products: 95.2 us -> 0 us
  between operations: 19.3 us -> 0.05 us
  blocking collectives: 0 us -> 13.8 us
    psum x2 -> x0, waiting for transfers between devices: 269 us -> none  [from_root(): return lax.psum(kept, axis)]
    pallas_call x0 -> x5, Pallas kernels: none -> 249 us  [the longest x1 99.9 us: factor_and_solve(): pl.pallas_call(factor_kernel, out_shape=(jax.ShapeDtypeStruct((B, LEAD),...]
    another operation x33 -> x0, other arithmetic: 237 us -> none  [the longest x29 159 us: body(): jnp.linalg.cholesky(jnp.tril(diag_block) + jnp.tril(diag_block, -1).T)]
    all_gather x4 -> x0, waiting for transfers between devices: 223 us -> none  [the longest x2 115 us: body(): lax.all_gather(solved_piece, 'tall', axis=0, tiled=True)]
    all_to_all x3 -> x2, waiting for transfers between devices: 167 us -> 46.8 us  [the longest x1 46.7 us: body(): lax.all_to_all(child_tiles, 'tall', split_axis=0, concat_axis=0, tiled=True)]
    dot_general x6 -> x0, matrix products: 72.3 us -> none  [the longest x2 34.8 us: body(): jnp.dot(lower_rows, column_rows.T, precision=full_precision, preferred_el...]
    gather x10 -> x0, local copies, waits for them, and re-layouts: 36.8 us -> none  [the longest x2 17.8 us: body(): jnp.take(new_diag, jnp.clip(global_row - low_row, 0, panel_width - 1), ax...]
    unnamed x34 -> x0, local copies, waits for them, and re-layouts: 24.5 us -> none
  transfers between devices with their start and end apart: 9 -> 2, of which waited for: 8 -> 1; matrix products, arithmetic and copies ran while one was open for 6% -> 0% of each run, Pallas kernels for 0% -> 55%
where the time goes in v1:
time: 332 us; the launch traced here: 331 us
  Pallas kernels  249 us (75%)
  waiting for transfers between devices  46.8 us (14%)
  starting transfers between devices  19.1 us (6%)
  blocking collectives  13.8 us (4%)
    pallas_call x1, Pallas kernels, factor_and_solve(): pl.pallas_call(factor_kernel, out_shape=(jax.ShapeDtypeStruct((B, LEAD),...  99.9 us
    pallas_call x1, Pallas kernels, share_solved(): pl.pallas_call(share_kernel, out_shape=(jax.ShapeDtypeStruct((16, B, LEAD...  82.8 us
    all_to_all x1, waiting for transfers between devices, body(): lax.all_to_all(child_tiles, 'tall', split_axis=0, concat_axis=0, tiled=True)  46.7 us
    pallas_call x1, Pallas kernels, share_lead(): pl.pallas_call(lead_kernel, out_shape=jax.ShapeDtypeStruct((LEAD // B, B,...  35.3 us
    pallas_call x1, Pallas kernels, update(): pl.pallas_call(update_kernel, grid=(total // chunk,), out_shape=jax.Shape...  19.8 us
    all_to_all x1, starting transfers between devices, body(): lax.all_to_all(slab, 'wide', split_axis=0, concat_axis=0, tiled=True)  14.5 us
    all_to_all x1, blocking collectives, body(): lax.all_to_all(child_targets[:, 1], 'tall', split_axis=0, concat_axis=0,...  13.8 us
    pallas_call x1, Pallas kernels, add_tiles(): pl.pallas_call(add_kernel, grid_spec=pltpu.PrefetchScalarGridSpec(num_sca...  11.1 us
  transfers between devices with their start and end apart: 2, of which 1 were waited for; matrix products, arithmetic and copies ran while one was open for 0% of the time, Pallas kernels for 55%

profile of v1, /device:TPU:1, one launch (start us, length us, event | category | flops | bytes accessed | tf_op | source)
XLA Modules:
  0.0 331.1 jit_solution(1562267015352465670)
XLA Ops:
  0.0 0.7 slice_reduce_fusion
  0.7 0.1 all_to_all.13
  0.8 13.8 %all_to_all.21 = s32[8,8,1]{1,2,0:T(1,128)S(1)} all-to-all(s32[8,8,1]{1,2,0:T(1,128)S(1)} %bitcast.9), channel_id=1, replica_groups=mesh['wide'=16,'tall'=8] {'tall'}, dimensions={0} | all-to-all | bytes 512 | tf_op jit(solution)/shard_map/all_to_all | solution.py:605
  14.6 4.5 %all-to-all-start.1 = ((f32[64,128,128]{2,1,0:T(8,128)}), f32[64,128,128]{2,1,0:T(8,128)}, u32[]{:S(2)}, u32[]{:S(2)}) async-start(f32[64,128,128]{2,1,0:T(8,128)} %param.4), calls=%async_computation.1 | async-start | bytes 8388608 | tf_op jit(solution)/shard_map/all_to_all | solution.py:606
  19.1 0.5 broadcast.6
  19.6 0.7 reduce.7
  20.3 0.7 all_to_all.15.cols_ref
  21.0 46.7 %all-to-all-done.1.tiles_ref = f32[64,128,128]{2,1,0:T(8,128)} async-done(((f32[64,128,128]{2,1,0:T(8,128)}), f32[64,128,128]{2,1,0:T(8,128)}, u32[]{:S(2)}, u32[]{:S(2)}) %all-to-all-start.1) | async-done | bytes 4194336 | tf_op jit(solution)/shard_map/all_to_all | solution.py:606
  67.7 11.1 %add_tiles.1 = (f32[16,128,1024]{2,1,0:T(8,128)}, f32[128,1024]{1,0:T(8,128)}) custom-call(s32[64]{0:T(128)} %all_to_all.15.cols_ref, f32[128,16384]{1,0:T(8,128)} %initial_ref.1, f32[64,128,128]{2,1,0:T(8,128)} %all-to-all-done.1.tiles_ref), custom_call_target="tpu_custom_call" | custom-call | tf_op jit(solution)/shard_map/add_tiles/pallas_call | solution.py:80
  78.8 35.3 %share_lead.1 = f32[8,128,1024]{2,1,0:T(8,128)} custom-call(f32[128,1024]{1,0:T(8,128)} %get-tuple-element.14.strip_ref), custom_call_target="tpu_custom_call" | custom-call | tf_op jit(solution)/shard_map/share_lead/pallas_call | solution.py:250
  114.1 14.5 %all-to-all-start.2 = ((f32[16,128,1024]{2,1,0:T(8,128)}), f32[16,128,1024]{2,1,0:T(8,128)}, u32[]{:S(2)}, u32[]{:S(2)}) async-start(f32[16,128,1024]{2,1,0:T(8,128)} %get-tuple-element.15), calls=%async_computation.2 | async-start | bytes 16777216 | tf_op jit(solution)/shard_map/all_to_all | solution.py:610
  128.6 99.9 %factor.1 = (f32[128,1024]{1,0:T(8,128)}, f32[128,1024]{1,0:T(8,128)}) custom-call(f32[1024,1024]{1,0:T(8,128)} %bitcast.6, f32[128,1024]{1,0:T(8,128)} %get-tuple-element.14.strip_ref), custom_call_target="tpu_custom_call" | custom-call | tf_op jit(solution)/shard_map/factor/pallas_call | solution.py:401
  228.5 82.8 %share_solved.1 = (f32[16,128,1024]{2,1,0:T(8,128)}, f32[8,128,1024]{2,1,0:T(8,128)}) custom-call(f32[128,1024]{1,0:T(8,128)} %get-tuple-element.17.mine_ref), custom_call_target="tpu_custom_call" | custom-call | tf_op jit(solution)/shard_map/share_solved/pallas_call | solution.py:533
  311.3 0.0 all-to-all-done.2
  311.3 19.8 %update.1 = f32[2048,1024]{1,0:T(8,128)} custom-call(f32[2048,1024]{1,0:T(8,128)} %bitcast.1.front_ref, f32[2048,1024]{1,0:T(8,128)} %bitcast.7, f32[1024,1024]{1,0:T(8,128)} %bitcast.8, f32[128,1024]{1,0:T(8,128)} %get-tuple-element.20.shown_ref), custom_call_target="tpu_custom_call" | custom-call | tf_op jit(solution)/shard_map/update/pallas_call | solution.py:586
Async XLA Ops:
  14.6 53.1 %all-to-all-start.1 = ((f32[64,128,128]{2,1,0:T(8,128)}), f32[64,128,128]{2,1,0:T(8,128)}, u32[]{:S(2)}, u32[]{:S(2)}) async-start(f32[64,128,128]{2,1,0:T(8,128)} %param.4), calls=%async_computation.1 | async-start | bytes 8388608 | tf_op jit(solution)/shard_map/all_to_all | solution.py:606
  114.1 197.2 %all-to-all-start.2 = ((f32[16,128,1024]{2,1,0:T(8,128)}), f32[16,128,1024]{2,1,0:T(8,128)}, u32[]{:S(2)}, u32[]{:S(2)}) async-start(f32[16,128,1024]{2,1,0:T(8,128)} %get-tuple-element.15), calls=%async_computation.2 | async-start | bytes 16777216 | tf_op jit(solution)/shard_map/all_to_all | solution.py:610

commit v2 on v1

--- a/solution.py
+++ b/solution.py
@@ -10,6 +10,7 @@
 PANEL = 512
 LEAD = 1024
 B = 128
+PADDED = LEAD + B
 MESH = pl.DeviceIdType.MESH
 NT = (((1,), (1,)), ((), ()))
 NN = (((1,), (0,)), ((), ()))
@@ -335,9 +336,32 @@
     return lax.dot_general(a, b, dims, precision=lax.Precision.HIGHEST, preferred_element_type=F32)
 
 
-def factor_lead(a, w, dblk, vblk, lcol):
-    n = a.shape[0]
+def thirds(x):
+    high = x.astype(jnp.bfloat16)
+    rest = x - high.astype(F32)
+    mid = rest.astype(jnp.bfloat16)
+    low = (rest - mid.astype(F32)).astype(jnp.bfloat16)
+    return high, mid, low
+
+
+def left6(x):
+    h, m, l = thirds(x)
+    return jnp.concatenate([h, m, h, m, h, l], axis=1)
+
+
+def right6(x, axis):
+    h, m, l = thirds(x)
+    return jnp.concatenate([h, h, m, m, l, h], axis=axis)
+
+
+def product(a, b, dims):
+    return lax.dot_general(a, b, dims, preferred_element_type=F32)
+
+
+def factor_lead(a, w, dblk, vblk, lleft, lright):
+    n = LEAD
     blocks = n // B
+    wide = 2 * B
     ri = lax.broadcasted_iota(jnp.int32, (B, B), 0)
     ci = lax.broadcasted_iota(jnp.int32, (B, B), 1)
     eye = jnp.where(ri == ci, 1.0, 0.0).astype(F32)
@@ -345,6 +369,9 @@
     wj = lax.broadcasted_iota(jnp.int32, (B, n), 1)
     for i in range(blocks):
         w[i * B : (i + 1) * B, :] = jnp.where(wi + i * B == wj, 1.0, 0.0)
+    w[n:, :] = jnp.zeros((B, n), F32)
+    a[0:n, n:] = jnp.zeros((n, B), F32)
+    a[n:, :] = jnp.zeros((B, n + B), F32)
 
     def step(j, carry):
         o = pl.multiple_of(j * B, B)
@@ -354,44 +381,64 @@
         factor_block(dblk, vblk)
         a[pl.ds(o, B), pl.ds(o, B)] = jnp.where(ri <= ci, dblk[...], 0.0).T
         winv = vblk[...]
-        wrow = dot6(winv, w[pl.ds(o, B), :], NN)
-        w[pl.ds(o, B), :] = wrow
-
-        def solve(i, c):
-            r = pl.multiple_of(i * B, B)
-            solved = dot6(a[pl.ds(r, B), pl.ds(o, B)], winv, NT)
-            a[pl.ds(r, B), pl.ds(o, B)] = solved
-            lcol[pl.ds(r, B), :] = solved
+        wright = right6(winv, 1)
+        wleft = left6(winv)
+        pairs = (blocks - j) // 2
+
+        def below(m):
+            return pl.multiple_of(o + B + m * wide, B)
+
+        def solve(m, c):
+            r = below(m)
+            solved = product(left6(a[pl.ds(r, wide), pl.ds(o, B)]), wright, NT)
+            a[pl.ds(r, wide), pl.ds(o, B)] = solved
+            lleft[pl.ds(r, wide), :] = left6(solved)
+            lright[pl.ds(r, wide), :] = right6(solved, 1)
             return c
 
-        lax.fori_loop(j + 1, blocks, solve, 0)
-
-        def update(i, c):
-            r = pl.multiple_of(i * B, B)
-            mine = lcol[pl.ds(r, B), :]
-            w[pl.ds(r, B), :] -= dot6(mine, wrow, NN)
-
-            def cols(k, cc):
-                s = pl.multiple_of(k * B, B)
-                a[pl.ds(r, B), pl.ds(s, B)] -= dot6(mine, lcol[pl.ds(s, B), :], NT)
+        lax.fori_loop(0, pairs, solve, 0)
+
+        def reduce(k, c):
+            at = pl.multiple_of(k * wide, wide)
+            wrow = product(wleft, right6(w[pl.ds(o, B), pl.ds(at, wide)], 0), NN)
+            w[pl.ds(o, B), pl.ds(at, wide)] = wrow
+            right = right6(wrow, 0)
+
+            def down(m, cc):
+                r = below(m)
+                w[pl.ds(r, wide), pl.ds(at, wide)] -= product(lleft[pl.ds(r, wide), :], right, NN)
                 return cc
 
-            lax.fori_loop(j + 1, i + 1, cols, 0)
+            lax.fori_loop(0, pairs, down, 0)
             return c
 
-        lax.fori_loop(j + 1, blocks, update, 0)
+        lax.fori_loop(0, j // 2 + 1, reduce, 0)
+
+        def update(k, c):
+            s = below(k)
+            right = lright[pl.ds(s, wide), :]
+
+            def down(m, cc):
+                r = below(m)
+                a[pl.ds(r, wide), pl.ds(s, wide)] -= product(lleft[pl.ds(r, wide), :], right, NT)
+                return cc
+
+            lax.fori_loop(k, pairs, down, 0)
+            return c
+
+        lax.fori_loop(0, pairs, update, 0)
         return carry
 
     lax.fori_loop(0, blocks, step, 0)
 
 
-def factor_kernel(lead_ref, strip_ref, solved_ref, shown_ref, a, w, dblk, vblk, lcol):
+def factor_kernel(lead_ref, strip_ref, solved_ref, shown_ref, a, w, dblk, vblk, lleft, lright):
     wide = lax.axis_index("wide")
     tall = lax.axis_index("tall")
-    a[...] = lead_ref[...]
-    factor_lead(a, w, dblk, vblk, lcol)
-    shown_ref[...] = a[pl.ds(pl.multiple_of(tall * B, B), B), :]
-    solved = dot6(strip_ref[...], w[...], NT)
+    a[0:LEAD, 0:LEAD] = lead_ref[...]
+    factor_lead(a, w, dblk, vblk, lleft, lright)
+    shown_ref[...] = a[pl.ds(pl.multiple_of(tall * B, B), B), 0:LEAD]
+    solved = dot6(strip_ref[...], w[0:LEAD, :], NT)
     cols = lax.broadcasted_iota(jnp.int32, solved.shape, 1)
     keep = (wide > 0) | ((tall >= PANEL // B) & (cols < PANEL))
     solved_ref[...] = jnp.where(keep, solved, 0.0)
@@ -404,35 +451,52 @@
         in_specs=[vmem_spec()] * 2,
         out_specs=(vmem_spec(),) * 2,
         scratch_shapes=[
-            pltpu.VMEM((LEAD, LEAD), F32),
-            pltpu.VMEM((LEAD, LEAD), F32),
+            pltpu.VMEM((PADDED, PADDED), F32),
+            pltpu.VMEM((PADDED, LEAD), F32),
             pltpu.VMEM((B, B), F32),
             pltpu.VMEM((B, B), F32),
-            pltpu.VMEM((LEAD, B), F32),
+            pltpu.VMEM((PADDED, 6 * B), jnp.bfloat16),
+            pltpu.VMEM((PADDED, 6 * B), jnp.bfloat16),
         ],
         compiler_params=params(),
         name="factor",
     )(lead, strip)
 
 
-def share_kernel(mine_ref, rows_ref, cols_ref, hold, send_sem, row_sem, col_sem, local_sem):
+def share_kernel(mine_ref, rows_ref, cols_ref, send_sem, row_sem, col_sem, local_sem):
     w, t, z, x, c, h, y = place()
     side = neighbours()
     half = B // 2
     target = 2 * lax.rem(w, 8) + h
     quarter = w // 8
-    partners = list(side.values())
-    greet(partners)
+    pair = w // 2
+    holder = h == c
+    away = target != w
+    barrier = pltpu.get_barrier_semaphore()
+    extra = [(away, target)] + [(holder & (q * 8 + pair != w), q * 8 + pair) for q in range(2)]
+    for partner in side.values():
+        pl.semaphore_signal(barrier, inc=1, device_id=partner, device_id_type=MESH)
+    for pred, k in extra:
+        @pl.when(pred)
+        def _():
+            pl.semaphore_signal(barrier, inc=1, device_id=(k, t), device_id_type=MESH)
+    peers = len(side)
+    for pred, _ in extra:
+        peers = peers + jnp.where(pred, 1, 0)
+    pl.semaphore_wait(barrier, peers)
     sent = []
     count = [0]
 
-    def push(ref, sem, to):
+    def copy_to(src, dst, sem, device):
         slot = count[0]
         count[0] += 1
         return pltpu.make_async_remote_copy(
-            src_ref=ref, dst_ref=ref, send_sem=send_sem.at[slot], recv_sem=sem,
-            device_id=side[to], device_id_type=MESH,
+            src_ref=src, dst_ref=dst, send_sem=send_sem.at[slot], recv_sem=sem,
+            device_id=device, device_id_type=MESH,
         )
+
+    def push(ref, sem, to):
+        return copy_to(ref, ref, sem, side[to])
 
     def go(copy, pred=None):
         if pred is None:
@@ -449,66 +513,57 @@
     def cpiece(q, i, n):
         return cols_ref.at[q * 4 + i, pl.ds(n * half, half), :]
 
+    def mpiece(n):
+        return mine_ref.at[pl.ds(n * half, half), :]
+
     own = pltpu.make_async_copy(mine_ref, rows_ref.at[w], local_sem.at[0])
     own.start()
-
-    def first(n, to):
-        slot = count[0]
-        count[0] += 1
-        return pltpu.make_async_remote_copy(
-            src_ref=mine_ref.at[pl.ds(n * half, half), :], dst_ref=rpiece(w, n),
-            send_sem=send_sem.at[slot], recv_sem=row_sem.at[w, n],
-            device_id=side[to], device_id_type=MESH,
-        )
+    kept = pltpu.make_async_copy(mine_ref, cols_ref.at[quarter * 4 + y], local_sem.at[1])
+
+    @pl.when(jnp.logical_not(away))
+    def _():
+        kept.start()
 
     for n in range(2):
+        go(copy_to(mpiece(n), cpiece(quarter, y, n), col_sem.at[quarter, y, n], (target, t)), away)
         for to in ("side", "up", "down", "core"):
-            go(first(n, to))
+            go(copy_to(mpiece(n), rpiece(w, n), row_sem.at[w, n], side[to]))
+
+    @pl.when(jnp.logical_not(away))
+    def _():
+        kept.wait()
+
     beside = wide_at(z, 1 - x, c)
     for n in range(2):
         arrived(rpiece(beside, n), row_sem.at[beside, n])
         for to in ("up", "down", "core"):
             go(push(rpiece(beside, n), row_sem.at[beside, n], to))
-    for xx in (x, 1 - x):
-        for n in range(2):
-            for dz, to, part in ((-1, "up", 0), (1, "down", 1)):
-                k = wide_at(z + dz, xx, c)
-                arrived(rpiece(k, n), row_sem.at[k, n])
-                if n == part:
-                    go(push(rpiece(k, n), row_sem.at[k, n], to))
-                go(push(rpiece(k, n), row_sem.at[k, n], "core"))
-    for xx in (x, 1 - x):
-        for n in range(2):
-            k = wide_at(z + 2, xx, c)
+
+    def take(q, n):
+        @pl.when(jnp.logical_not(holder) | (q * 8 + pair != w))
+        def _():
+            arrived(cpiece(q, y, n), col_sem.at[q, y, n])
+
+        go(push(cpiece(q, y, n), col_sem.at[q, y, n], "far"), holder)
+        go(push(cpiece(q, y, n), col_sem.at[q, y, n], "north"))
+        go(push(cpiece(q, y, n), col_sem.at[q, y, n], "south"))
+
+    def next_rows(xx, n):
+        for dz, to, part in ((-1, "up", 0), (1, "down", 1)):
+            k = wide_at(z + dz, xx, c)
             arrived(rpiece(k, n), row_sem.at[k, n])
+            if n == part:
+                go(push(rpiece(k, n), row_sem.at[k, n], to))
             go(push(rpiece(k, n), row_sem.at[k, n], "core"))
-    for zz in (z, z - 1, z + 1, z + 2):
-        for xx in (x, 1 - x):
-            k = wide_at(zz, xx, 1 - c)
-            for n in range(2):
-                arrived(rpiece(k, n), row_sem.at[k, n])
-    own.wait()
-    pair = w // 2
-    holder = h == c
+
     for q in range(2):
-        k = q * 8 + pair
-
-        @pl.when(holder)
-        def _():
-            take = pltpu.make_async_copy(rows_ref.at[k], hold.at[q], local_sem.at[1])
-            take.start()
-            take.wait()
-            put = pltpu.make_async_copy(hold.at[q], cols_ref.at[q * 4 + y], local_sem.at[1])
-            put.start()
-            put.wait()
+        take(q, 0)
+    for n in range(2):
+        next_rows(x, n)
     for q in range(2):
-        for n in range(2):
-            @pl.when(jnp.logical_not(holder))
-            def _():
-                arrived(cpiece(q, y, n), col_sem.at[q, y, n])
-            go(push(cpiece(q, y, n), col_sem.at[q, y, n], "far"), holder)
-            go(push(cpiece(q, y, n), col_sem.at[q, y, n], "north"))
-            go(push(cpiece(q, y, n), col_sem.at[q, y, n], "south"))
+        take(q, 1)
+    for n in range(2):
+        next_rows(1 - x, n)
     for q in range(2):
         for n in range(2):
             for dy, to, part in ((-1, "north", 0), (1, "south", 1)):
@@ -516,10 +571,21 @@
                 arrived(cpiece(q, i, n), col_sem.at[q, i, n])
                 if n == part:
                     go(push(cpiece(q, i, n), col_sem.at[q, i, n], to))
+    for xx in (x, 1 - x):
+        for n in range(2):
+            k = wide_at(z + 2, xx, c)
+            arrived(rpiece(k, n), row_sem.at[k, n])
+            go(push(rpiece(k, n), row_sem.at[k, n], "core"))
     for q in range(2):
         for n in range(2):
             i = lax.rem(y + 2, 4)
             arrived(cpiece(q, i, n), col_sem.at[q, i, n])
+    for zz in (z, z - 1, z + 1, z + 2):
+        for xx in (x, 1 - x):
+            k = wide_at(zz, xx, 1 - c)
+            for n in range(2):
+                arrived(rpiece(k, n), row_sem.at[k, n])
+    own.wait()
     for pred, copy in sent:
         if pred is None:
             copy.wait_send()
@@ -539,7 +605,6 @@
         in_specs=[vmem_spec()],
         out_specs=(any_spec(), any_spec()),
         scratch_shapes=[
-            pltpu.VMEM((2, B, LEAD), F32),
             pltpu.SemaphoreType.DMA((64,)),
             pltpu.SemaphoreType.DMA((16, 2)),
             pltpu.SemaphoreType.DMA((2, 4, 2)),

time: 332 us -> 298 us (0.90)
  Pallas kernels: 249 us -> 215 us
    pallas_call x1, Pallas kernels: 99.9 us -> 72.7 us  [factor_and_solve(): pl.pallas_call(factor_kernel, out_shape=(jax.ShapeDtypeStruct((B, LEAD),...]
    pallas_call x1, Pallas kernels: 82.8 us -> 76 us  [share_solved(): pl.pallas_call(share_kernel, out_shape=(jax.ShapeDtypeStruct((16, B, LEAD...]
  transfers between devices with their start and end apart: 2 -> 2, of which waited for: 1 -> 1; matrix products, arithmetic and copies ran while one was open for 0% -> 0% of each run, Pallas kernels for 55% -> 50%
where the time goes in v2:
time: 298 us; the launch traced here: 297 us
  Pallas kernels  215 us (72%)
  waiting for transfers between devices  46.8 us (16%)
  starting transfers between devices  19.1 us (6%)
  blocking collectives  13.8 us (5%)
    pallas_call x1, Pallas kernels, share_solved(): pl.pallas_call(share_kernel, out_shape=(jax.ShapeDtypeStruct((16, B, LEAD...  76 us
    pallas_call x1, Pallas kernels, factor_and_solve(): pl.pallas_call(factor_kernel, out_shape=(jax.ShapeDtypeStruct((B, LEAD),...  72.7 us
    all_to_all x1, waiting for transfers between devices, body(): lax.all_to_all(child_tiles, 'tall', split_axis=0, concat_axis=0, tiled=True)  46.7 us
    pallas_call x1, Pallas kernels, share_lead(): pl.pallas_call(lead_kernel, out_shape=jax.ShapeDtypeStruct((LEAD // B, B,...  35.3 us
    pallas_call x1, Pallas kernels, update(): pl.pallas_call(update_kernel, grid=(total // chunk,), out_shape=jax.Shape...  19.8 us
    all_to_all x1, starting transfers between devices, body(): lax.all_to_all(slab, 'wide', split_axis=0, concat_axis=0, tiled=True)  14.5 us
    all_to_all x1, blocking collectives, body(): lax.all_to_all(child_targets[:, 1], 'tall', split_axis=0, concat_axis=0,...  13.8 us
    pallas_call x1, Pallas kernels, add_tiles(): pl.pallas_call(add_kernel, grid_spec=pltpu.PrefetchScalarGridSpec(num_sca...  11.1 us
  transfers between devices with their start and end apart: 2, of which 1 were waited for; matrix products, arithmetic and copies ran while one was open for 0% of the time, Pallas kernels for 50%

profile of v2, /device:TPU:1, one launch (start us, length us, event | category | flops | bytes accessed | tf_op | source)
XLA Modules:
  0.0 297.2 jit_solution(18328993130022909542)
XLA Ops:
  0.0 0.7 slice_reduce_fusion
  0.7 0.1 all_to_all.13
  0.8 13.8 %all_to_all.21 = s32[8,8,1]{1,2,0:T(1,128)S(1)} all-to-all(s32[8,8,1]{1,2,0:T(1,128)S(1)} %bitcast.9), channel_id=1, replica_groups=mesh['wide'=16,'tall'=8] {'tall'}, dimensions={0} | all-to-all | bytes 512 | tf_op jit(solution)/shard_map/all_to_all | solution.py:670
  14.6 4.5 %all-to-all-start.1 = ((f32[64,128,128]{2,1,0:T(8,128)}), f32[64,128,128]{2,1,0:T(8,128)}, u32[]{:S(2)}, u32[]{:S(2)}) async-start(f32[64,128,128]{2,1,0:T(8,128)} %param.4), calls=%async_computation.1 | async-start | bytes 8388608 | tf_op jit(solution)/shard_map/all_to_all | solution.py:671
  19.1 0.5 broadcast.6
  19.6 0.7 reduce.7
  20.3 0.7 all_to_all.15.cols_ref
  21.0 46.7 %all-to-all-done.1.tiles_ref = f32[64,128,128]{2,1,0:T(8,128)} async-done(((f32[64,128,128]{2,1,0:T(8,128)}), f32[64,128,128]{2,1,0:T(8,128)}, u32[]{:S(2)}, u32[]{:S(2)}) %all-to-all-start.1) | async-done | bytes 4194336 | tf_op jit(solution)/shard_map/all_to_all | solution.py:671
  67.7 11.1 %add_tiles.1 = (f32[16,128,1024]{2,1,0:T(8,128)}, f32[128,1024]{1,0:T(8,128)}) custom-call(s32[64]{0:T(128)} %all_to_all.15.cols_ref, f32[128,16384]{1,0:T(8,128)} %initial_ref.1, f32[64,128,128]{2,1,0:T(8,128)} %all-to-all-done.1.tiles_ref), custom_call_target="tpu_custom_call" | custom-call | tf_op jit(solution)/shard_map/add_tiles/pallas_call | solution.py:81
  78.8 35.3 %share_lead.1 = f32[8,128,1024]{2,1,0:T(8,128)} custom-call(f32[128,1024]{1,0:T(8,128)} %get-tuple-element.14.strip_ref), custom_call_target="tpu_custom_call" | custom-call | tf_op jit(solution)/shard_map/share_lead/pallas_call | solution.py:251
  114.1 14.5 %all-to-all-start.2 = ((f32[16,128,1024]{2,1,0:T(8,128)}), f32[16,128,1024]{2,1,0:T(8,128)}, u32[]{:S(2)}, u32[]{:S(2)}) async-start(f32[16,128,1024]{2,1,0:T(8,128)} %get-tuple-element.15), calls=%async_computation.2 | async-start | bytes 16777216 | tf_op jit(solution)/shard_map/all_to_all | solution.py:675
  128.6 72.7 %factor.1 = (f32[128,1024]{1,0:T(8,128)}, f32[128,1024]{1,0:T(8,128)}) custom-call(f32[1024,1024]{1,0:T(8,128)} %bitcast.6, f32[128,1024]{1,0:T(8,128)} %get-tuple-element.14.strip_ref), custom_call_target="tpu_custom_call" | custom-call | tf_op jit(solution)/shard_map/factor/pallas_call | solution.py:448
  201.4 76.0 %share_solved.1 = (f32[16,128,1024]{2,1,0:T(8,128)}, f32[8,128,1024]{2,1,0:T(8,128)}) custom-call(f32[128,1024]{1,0:T(8,128)} %get-tuple-element.17.mine_ref), custom_call_target="tpu_custom_call" | custom-call | tf_op jit(solution)/shard_map/share_solved/pallas_call | solution.py:599
  277.3 0.0 all-to-all-done.2
  277.4 19.8 %update.1 = f32[2048,1024]{1,0:T(8,128)} custom-call(f32[2048,1024]{1,0:T(8,128)} %bitcast.1.front_ref, f32[2048,1024]{1,0:T(8,128)} %bitcast.7, f32[1024,1024]{1,0:T(8,128)} %bitcast.8, f32[128,1024]{1,0:T(8,128)} %get-tuple-element.20.shown_ref), custom_call_target="tpu_custom_call" | custom-call | tf_op jit(solution)/shard_map/update/pallas_call | solution.py:651
Async XLA Ops:
  14.6 53.1 %all-to-all-start.1 = ((f32[64,128,128]{2,1,0:T(8,128)}), f32[64,128,128]{2,1,0:T(8,128)}, u32[]{:S(2)}, u32[]{:S(2)}) async-start(f32[64,128,128]{2,1,0:T(8,128)} %param.4), calls=%async_computation.1 | async-start | bytes 8388608 | tf_op jit(solution)/shard_map/all_to_all | solution.py:671
  114.1 163.2 %all-to-all-start.2 = ((f32[16,128,1024]{2,1,0:T(8,128)}), f32[16,128,1024]{2,1,0:T(8,128)}, u32[]{:S(2)}, u32[]{:S(2)}) async-start(f32[16,128,1024]{2,1,0:T(8,128)} %get-tuple-element.15), calls=%async_computation.2 | async-start | bytes 16777216 | tf_op jit(solution)/shard_map/all_to_all | solution.py:675

commit v3 on v2

--- a/solution.py
+++ b/solution.py
@@ -150,6 +150,43 @@
 
 def arrived(ref, sem):
     pltpu.make_async_copy(ref, ref, sem).wait()
+
+
+def cols_kernel(src_ref, out_ref, send_sem, recv_sem, local_sem):
+    w, t = lax.axis_index("wide"), lax.axis_index("tall")
+    talls = src_ref.shape[0]
+    greet([(w, lax.rem(t + d, talls)) for d in range(1, talls)])
+    own = pltpu.make_async_copy(src_ref.at[t], out_ref.at[t], local_sem)
+    own.start()
+    sent = []
+    for d in range(1, talls):
+        to = lax.rem(t + d, talls)
+        sent.append(send(src_ref.at[to], out_ref.at[t], send_sem.at[d], recv_sem.at[t], (w, to)))
+    for d in range(1, talls):
+        source = lax.rem(t + talls - d, talls)
+        arrived(out_ref.at[source], recv_sem.at[source])
+    own.wait()
+    for copy in sent:
+        copy.wait_send()
+
+
+def share_cols(cols, talls):
+    each = cols.shape[0] // talls
+    padded = jnp.pad(cols.reshape(talls, 1, each), ((0, 0), (0, 7), (0, B - each)))
+    got = pl.pallas_call(
+        cols_kernel,
+        out_shape=jax.ShapeDtypeStruct(padded.shape, padded.dtype),
+        in_specs=[vmem_spec()],
+        out_specs=vmem_spec(),
+        scratch_shapes=[
+            pltpu.SemaphoreType.DMA((talls,)),
+            pltpu.SemaphoreType.DMA((talls,)),
+            pltpu.SemaphoreType.DMA,
+        ],
+        compiler_params=params(collective_id=2, has_side_effects=True),
+        name="share_cols",
+    )(padded)
+    return got[:, 0, :each].reshape(-1)
 
 
 CHUNKS = 4
@@ -667,11 +704,10 @@
 
 def body(initial, child_tiles, child_targets):
     wides = lax.axis_size("wide")
-    cols = lax.all_to_all(child_targets[:, 1], "tall", split_axis=0, concat_axis=0, tiled=True)
+    cols = share_cols(child_targets[:, 1], lax.axis_size("tall"))
     tiles = lax.all_to_all(child_tiles, "tall", split_axis=0, concat_axis=0, tiled=True)
     slab, strip = add_tiles(initial, tiles, cols, wides)
     lead = share_lead(strip)
-    slab, lead = lax.optimization_barrier((slab, lead))
     front = lax.all_to_all(slab, "wide", split_axis=0, concat_axis=0, tiled=True)
     solved, shown = factor_and_solve(lead.reshape(LEAD, LEAD), strip)
     rows, columns = share_solved(solved)

time: 298 us -> 357 us (1.20)
  Pallas kernels: 215 us -> 338 us
  waiting for transfers between devices: 46.8 us -> 0.01 us
  blocking collectives: 13.8 us -> 0 us
  starting transfers between devices: 19.1 us -> 15.3 us
    pallas_call x1, Pallas kernels: 35.3 us -> 119 us  [share_lead(): pl.pallas_call(lead_kernel, out_shape=jax.ShapeDtypeStruct((LEAD // B, B,...]
    pallas_call x0 -> x1, Pallas kernels: none -> 50.3 us  [share_cols(): pl.pallas_call(cols_kernel, out_shape=jax.ShapeDtypeStruct(padded.shape,...]
    all_to_all x1, waiting for transfers between devices: 46.7 us -> 0.01 us  [body(): lax.all_to_all(child_tiles, 'tall', split_axis=0, concat_axis=0, tiled=True)]
    all_to_all x1 -> x0, blocking collectives: 13.8 us -> none  [body(): lax.all_to_all(child_targets[:, 1], 'tall', split_axis=0, concat_axis=0,...]
    pallas_call x1, Pallas kernels: 76 us -> 65.8 us  [share_solved(): pl.pallas_call(share_kernel, out_shape=(jax.ShapeDtypeStruct((16, B, LEAD...]
    all_to_all x1, starting transfers between devices: 14.5 us -> 7.66 us  [body(): lax.all_to_all(slab, 'wide', split_axis=0, concat_axis=0, tiled=True)]
  transfers between devices with their start and end apart: 2 -> 2, of which waited for: 1 -> 0; matrix products, arithmetic and copies ran while one was open for 0% -> 1% of each run, Pallas kernels for 50% -> 86%
where the time goes in v3:
time: 357 us; the launch traced here: 356 us
  Pallas kernels  338 us (95%)
  starting transfers between devices  15.3 us (4%)
    pallas_call x1, Pallas kernels, share_lead(): pl.pallas_call(lead_kernel, out_shape=jax.ShapeDtypeStruct((LEAD // B, B,...  119 us
    pallas_call x1, Pallas kernels, factor_and_solve(): pl.pallas_call(factor_kernel, out_shape=(jax.ShapeDtypeStruct((B, LEAD),...  72.8 us
    pallas_call x1, Pallas kernels, share_solved(): pl.pallas_call(share_kernel, out_shape=(jax.ShapeDtypeStruct((16, B, LEAD...  65.8 us
    pallas_call x1, Pallas kernels, share_cols(): pl.pallas_call(cols_kernel, out_shape=jax.ShapeDtypeStruct(padded.shape,...  50.3 us
    pallas_call x1, Pallas kernels, update(): pl.pallas_call(update_kernel, grid=(total // chunk,), out_shape=jax.Shape...  19.8 us
    pallas_call x1, Pallas kernels, add_tiles(): pl.pallas_call(add_kernel, grid_spec=pltpu.PrefetchScalarGridSpec(num_sca...  11.1 us
    all_to_all x1, starting transfers between devices, body(): lax.all_to_all(slab, 'wide', split_axis=0, concat_axis=0, tiled=True)  7.66 us
    all_to_all x1, starting transfers between devices, body(): lax.all_to_all(child_tiles, 'tall', split_axis=0, concat_axis=0, tiled=True)  7.61 us
  transfers between devices with their start and end apart: 2, of which 0 were waited for; matrix products, arithmetic and copies ran while one was open for 1% of the time, Pallas kernels for 86%

profile of v3, /device:TPU:1, one launch (start us, length us, event | category | flops | bytes accessed | tf_op | source)
XLA Modules:
  0.0 355.7 jit_solution(7103179773824261529)
XLA Ops:
  0.0 0.0 copy-start
  0.0 7.6 %all-to-all-start = ((f32[64,128,128]{2,1,0:T(8,128)}), f32[64,128,128]{2,1,0:T(8,128)}, u32[]{:S(2)}, u32[]{:S(2)}) async-start(f32[64,128,128]{2,1,0:T(8,128)} %param.4), calls=%async_computation | async-start | bytes 8388608 | tf_op jit(solution)/shard_map/all_to_all | solution.py:708
  7.6 0.0 copy-done
  7.6 0.1 reshape_squeeze.6
  7.7 0.6 pad.4.src_ref
  8.3 50.3 %share_cols.1 = s32[8,8,128]{2,1,0:T(8,128)} custom-call(s32[8,8,128]{2,1,0:T(8,128)} %pad.4.src_ref), custom_call_target="tpu_custom_call" | custom-call | tf_op jit(solution)/shard_map/share_cols/pallas_call | solution.py:176
  58.6 0.8 slice_reduce_fusion
  59.4 0.6 reshape_squeeze.7.cols_ref
  60.0 0.0 all-to-all-done.tiles_ref
  60.0 11.1 %add_tiles.1 = (f32[16,128,1024]{2,1,0:T(8,128)}, f32[128,1024]{1,0:T(8,128)}) custom-call(s32[64]{0:T(128)} %reshape_squeeze.7.cols_ref, f32[128,16384]{1,0:T(8,128)} %initial_ref.1, f32[64,128,128]{2,1,0:T(8,128)} %all-to-all-done.tiles_ref), custom_call_target="tpu_custom_call" | custom-call | tf_op jit(solution)/shard_map/add_tiles/pallas_call | solution.py:81
  71.1 7.7 %all-to-all-start.1 = ((f32[16,128,1024]{2,1,0:T(8,128)}), f32[16,128,1024]{2,1,0:T(8,128)}, u32[]{:S(2)}, u32[]{:S(2)}) async-start(f32[16,128,1024]{2,1,0:T(8,128)} %get-tuple-element.11), calls=%async_computation.1 | async-start | bytes 16777216 | tf_op jit(solution)/shard_map/all_to_all | solution.py:711
  78.8 118.6 %share_lead.1 = f32[8,128,1024]{2,1,0:T(8,128)} custom-call(f32[128,1024]{1,0:T(8,128)} %get-tuple-element.12.strip_ref), custom_call_target="tpu_custom_call" | custom-call | tf_op jit(solution)/shard_map/share_lead/pallas_call | solution.py:288
  197.3 72.8 %factor.1 = (f32[128,1024]{1,0:T(8,128)}, f32[128,1024]{1,0:T(8,128)}) custom-call(f32[1024,1024]{1,0:T(8,128)} %bitcast.5, f32[128,1024]{1,0:T(8,128)} %get-tuple-element.12.strip_ref), custom_call_target="tpu_custom_call" | custom-call | tf_op jit(solution)/shard_map/factor/pallas_call | solution.py:485
  270.1 65.8 %share_solved.1 = (f32[16,128,1024]{2,1,0:T(8,128)}, f32[8,128,1024]{2,1,0:T(8,128)}) custom-call(f32[128,1024]{1,0:T(8,128)} %get-tuple-element.13.mine_ref), custom_call_target="tpu_custom_call" | custom-call | tf_op jit(solution)/shard_map/share_solved/pallas_call | solution.py:636
  335.9 0.0 all-to-all-done.1
  335.9 19.8 %update.1 = f32[2048,1024]{1,0:T(8,128)} custom-call(f32[2048,1024]{1,0:T(8,128)} %bitcast.1.front_ref, f32[2048,1024]{1,0:T(8,128)} %bitcast.6, f32[1024,1024]{1,0:T(8,128)} %bitcast.7, f32[128,1024]{1,0:T(8,128)} %get-tuple-element.16.shown_ref), custom_call_target="tpu_custom_call" | custom-call | tf_op jit(solution)/shard_map/update/pallas_call | solution.py:688
  (1 shorter events, 0.0 us)
Async XLA Ops:
  0.0 7.6 %copy-start = (s32[64,2]{0,1:T(2,128)S(1)}, s32[64,2]{0,1:T(2,128)}, u32[]{:S(2)}) copy-start(s32[64,2]{0,1:T(2,128)} %param.5) | copy-start | bytes 1540
  0.0 60.0 %all-to-all-start = ((f32[64,128,128]{2,1,0:T(8,128)}), f32[64,128,128]{2,1,0:T(8,128)}, u32[]{:S(2)}, u32[]{:S(2)}) async-start(f32[64,128,128]{2,1,0:T(8,128)} %param.4), calls=%async_computation | async-start | bytes 8388608 | tf_op jit(solution)/shard_map/all_to_all | solution.py:708
  71.1 264.8 %all-to-all-start.1 = ((f32[16,128,1024]{2,1,0:T(8,128)}), f32[16,128,1024]{2,1,0:T(8,128)}, u32[]{:S(2)}, u32[]{:S(2)}) async-start(f32[16,128,1024]{2,1,0:T(8,128)} %get-tuple-element.11), calls=%async_computation.1 | async-start | bytes 16777216 | tf_op jit(solution)/shard_map/all_to_all | solution.py:711

commit v4 on v3

--- a/solution.py
+++ b/solution.py
@@ -10,10 +10,10 @@
 PANEL = 512
 LEAD = 1024
 B = 128
-PADDED = LEAD + B
+ROWS = LEAD + 2 * B
+COLS = LEAD + B
 MESH = pl.DeviceIdType.MESH
 NT = (((1,), (1,)), ((), ()))
-NN = (((1,), (0,)), ((), ()))
 VMEM_LIMIT = 60 * 1024 * 1024
 F32 = jnp.float32
 
@@ -369,10 +369,6 @@
     return d(a[0], b[0]) + (d(a[0], b[1]) + d(a[1], b[0]))
 
 
-def dot6(a, b, dims):
-    return lax.dot_general(a, b, dims, precision=lax.Precision.HIGHEST, preferred_element_type=F32)
-
-
 def thirds(x):
     high = x.astype(jnp.bfloat16)
     rest = x - high.astype(F32)
@@ -395,20 +391,14 @@
     return lax.dot_general(a, b, dims, preferred_element_type=F32)
 
 
-def factor_lead(a, w, dblk, vblk, lleft, lright):
-    n = LEAD
-    blocks = n // B
+def factor_lead(a, dblk, vblk, lleft, lright):
+    blocks = LEAD // B
     wide = 2 * B
     ri = lax.broadcasted_iota(jnp.int32, (B, B), 0)
     ci = lax.broadcasted_iota(jnp.int32, (B, B), 1)
     eye = jnp.where(ri == ci, 1.0, 0.0).astype(F32)
-    wi = lax.broadcasted_iota(jnp.int32, (B, n), 0)
-    wj = lax.broadcasted_iota(jnp.int32, (B, n), 1)
-    for i in range(blocks):
-        w[i * B : (i + 1) * B, :] = jnp.where(wi + i * B == wj, 1.0, 0.0)
-    w[n:, :] = jnp.zeros((B, n), F32)
-    a[0:n, n:] = jnp.zeros((n, B), F32)
-    a[n:, :] = jnp.zeros((B, n + B), F32)
+    a[LEAD + B :, :] = jnp.zeros((ROWS - LEAD - B, COLS), F32)
+    a[0 : LEAD + B, LEAD:] = jnp.zeros((LEAD + B, COLS - LEAD), F32)
 
     def step(j, carry):
         o = pl.multiple_of(j * B, B)
@@ -417,39 +407,22 @@
         vblk[...] = eye
         factor_block(dblk, vblk)
         a[pl.ds(o, B), pl.ds(o, B)] = jnp.where(ri <= ci, dblk[...], 0.0).T
-        winv = vblk[...]
-        wright = right6(winv, 1)
-        wleft = left6(winv)
-        pairs = (blocks - j) // 2
+        inverse = right6(vblk[...], 1)
+        row_pairs = (blocks - j + 1) // 2
+        col_pairs = (blocks - j) // 2
 
         def below(m):
             return pl.multiple_of(o + B + m * wide, B)
 
         def solve(m, c):
             r = below(m)
-            solved = product(left6(a[pl.ds(r, wide), pl.ds(o, B)]), wright, NT)
+            solved = product(left6(a[pl.ds(r, wide), pl.ds(o, B)]), inverse, NT)
             a[pl.ds(r, wide), pl.ds(o, B)] = solved
             lleft[pl.ds(r, wide), :] = left6(solved)
             lright[pl.ds(r, wide), :] = right6(solved, 1)
             return c
 
-        lax.fori_loop(0, pairs, solve, 0)
-
-        def reduce(k, c):
-            at = pl.multiple_of(k * wide, wide)
-            wrow = product(wleft, right6(w[pl.ds(o, B), pl.ds(at, wide)], 0), NN)
-            w[pl.ds(o, B), pl.ds(at, wide)] = wrow
-            right = right6(wrow, 0)
-
-            def down(m, cc):
-                r = below(m)
-                w[pl.ds(r, wide), pl.ds(at, wide)] -= product(lleft[pl.ds(r, wide), :], right, NN)
-                return cc
-
-            lax.fori_loop(0, pairs, down, 0)
-            return c
-
-        lax.fori_loop(0, j // 2 + 1, reduce, 0)
+        lax.fori_loop(0, row_pairs, solve, 0)
 
         def update(k, c):
             s = below(k)
@@ -460,22 +433,23 @@
                 a[pl.ds(r, wide), pl.ds(s, wide)] -= product(lleft[pl.ds(r, wide), :], right, NT)
                 return cc
 
-            lax.fori_loop(k, pairs, down, 0)
+            lax.fori_loop(k, row_pairs, down, 0)
             return c
 
-        lax.fori_loop(0, pairs, update, 0)
+        lax.fori_loop(0, col_pairs, update, 0)
         return carry
 
     lax.fori_loop(0, blocks, step, 0)
 
 
-def factor_kernel(lead_ref, strip_ref, solved_ref, shown_ref, a, w, dblk, vblk, lleft, lright):
+def factor_kernel(lead_ref, strip_ref, solved_ref, shown_ref, a, dblk, vblk, lleft, lright):
     wide = lax.axis_index("wide")
     tall = lax.axis_index("tall")
     a[0:LEAD, 0:LEAD] = lead_ref[...]
-    factor_lead(a, w, dblk, vblk, lleft, lright)
+    a[LEAD : LEAD + B, 0:LEAD] = strip_ref[...]
+    factor_lead(a, dblk, vblk, lleft, lright)
     shown_ref[...] = a[pl.ds(pl.multiple_of(tall * B, B), B), 0:LEAD]
-    solved = dot6(strip_ref[...], w[0:LEAD, :], NT)
+    solved = a[LEAD : LEAD + B, 0:LEAD]
     cols = lax.broadcasted_iota(jnp.int32, solved.shape, 1)
     keep = (wide > 0) | ((tall >= PANEL // B) & (cols < PANEL))
     solved_ref[...] = jnp.where(keep, solved, 0.0)
@@ -488,12 +462,11 @@
         in_specs=[vmem_spec()] * 2,
         out_specs=(vmem_spec(),) * 2,
         scratch_shapes=[
-            pltpu.VMEM((PADDED, PADDED), F32),
-            pltpu.VMEM((PADDED, LEAD), F32),
+            pltpu.VMEM((ROWS, COLS), F32),
             pltpu.VMEM((B, B), F32),
             pltpu.VMEM((B, B), F32),
-            pltpu.VMEM((PADDED, 6 * B), jnp.bfloat16),
-            pltpu.VMEM((PADDED, 6 * B), jnp.bfloat16),
+            pltpu.VMEM((ROWS, 6 * B), jnp.bfloat16),
+            pltpu.VMEM((ROWS, 6 * B), jnp.bfloat16),
         ],
         compiler_params=params(),
         name="factor",
@@ -708,6 +681,7 @@
     tiles = lax.all_to_all(child_tiles, "tall", split_axis=0, concat_axis=0, tiled=True)
     slab, strip = add_tiles(initial, tiles, cols, wides)
     lead = share_lead(strip)
+    slab, lead = lax.optimization_barrier((slab, lead))
     front = lax.all_to_all(slab, "wide", split_axis=0, concat_axis=0, tiled=True)
     solved, shown = factor_and_solve(lead.reshape(LEAD, LEAD), strip)
     rows, columns = share_solved(solved)

time: 357 us -> 290 us (0.81)
  Pallas kernels: 338 us -> 264 us
  starting transfers between devices: 15.3 us -> 22.7 us
    pallas_call x1, Pallas kernels: 119 us -> 34.1 us  [share_lead(): pl.pallas_call(lead_kernel, out_shape=jax.ShapeDtypeStruct((LEAD // B, B,...]
    pallas_call x1, Pallas kernels: 65.8 us -> 90.7 us  [share_solved(): pl.pallas_call(share_kernel, out_shape=(jax.ShapeDtypeStruct((16, B, LEAD...]
    pallas_call x1, Pallas kernels: 72.8 us -> 58.4 us  [factor_and_solve(): pl.pallas_call(factor_kernel, out_shape=(jax.ShapeDtypeStruct((B, LEAD),...]
    all_to_all x1, starting transfers between devices: 7.66 us -> 15 us  [body(): lax.all_to_all(slab, 'wide', split_axis=0, concat_axis=0, tiled=True)]
  transfers between devices with their start and end apart: 2 -> 2, of which waited for: 0 -> 0; matrix products, arithmetic and copies ran while one was open for 1% -> 1% of each run, Pallas kernels for 86% -> 69%
where the time goes in v4:
time: 290 us; the launch traced here: 289 us
  Pallas kernels  264 us (91%)
  starting transfers between devices  22.7 us (8%)
    pallas_call x1, Pallas kernels, share_solved(): pl.pallas_call(share_kernel, out_shape=(jax.ShapeDtypeStruct((16, B, LEAD...  90.7 us
    pallas_call x1, Pallas kernels, factor_and_solve(): pl.pallas_call(factor_kernel, out_shape=(jax.ShapeDtypeStruct((B, LEAD),...  58.4 us
    pallas_call x1, Pallas kernels, share_cols(): pl.pallas_call(cols_kernel, out_shape=jax.ShapeDtypeStruct(padded.shape,...  50.3 us
    pallas_call x1, Pallas kernels, share_lead(): pl.pallas_call(lead_kernel, out_shape=jax.ShapeDtypeStruct((LEAD // B, B,...  34.1 us
    pallas_call x1, Pallas kernels, update(): pl.pallas_call(update_kernel, grid=(total // chunk,), out_shape=jax.Shape...  19.8 us
    all_to_all x1, starting transfers between devices, body(): lax.all_to_all(slab, 'wide', split_axis=0, concat_axis=0, tiled=True)  15 us
    pallas_call x1, Pallas kernels, add_tiles(): pl.pallas_call(add_kernel, grid_spec=pltpu.PrefetchScalarGridSpec(num_sca...  11.1 us
    all_to_all x1, starting transfers between devices, body(): lax.all_to_all(child_tiles, 'tall', split_axis=0, concat_axis=0, tiled=True)  7.61 us
  transfers between devices with their start and end apart: 2, of which 0 were waited for; matrix products, arithmetic and copies ran while one was open for 1% of the time, Pallas kernels for 69%

profile of v4, /device:TPU:1, one launch (start us, length us, event | category | flops | bytes accessed | tf_op | source)
XLA Modules:
  0.0 289.2 jit_solution(7591878813470345617)
XLA Ops:
  0.0 0.0 copy-start
  0.0 7.6 %all-to-all-start = ((f32[64,128,128]{2,1,0:T(8,128)}), f32[64,128,128]{2,1,0:T(8,128)}, u32[]{:S(2)}, u32[]{:S(2)}) async-start(f32[64,128,128]{2,1,0:T(8,128)} %param.4), calls=%async_computation | async-start | bytes 8388608 | tf_op jit(solution)/shard_map/all_to_all | solution.py:681
  7.6 0.0 copy-done
  7.6 0.1 reshape_squeeze.6
  7.7 0.6 pad.4.src_ref
  8.3 50.3 %share_cols.1 = s32[8,8,128]{2,1,0:T(8,128)} custom-call(s32[8,8,128]{2,1,0:T(8,128)} %pad.4.src_ref), custom_call_target="tpu_custom_call" | custom-call | tf_op jit(solution)/shard_map/share_cols/pallas_call | solution.py:176
  58.6 0.8 slice_reduce_fusion
  59.4 0.6 reshape_squeeze.7.cols_ref
  60.0 0.0 all-to-all-done.tiles_ref
  60.0 11.1 %add_tiles.1 = (f32[16,128,1024]{2,1,0:T(8,128)}, f32[128,1024]{1,0:T(8,128)}) custom-call(s32[64]{0:T(128)} %reshape_squeeze.7.cols_ref, f32[128,16384]{1,0:T(8,128)} %initial_ref.1, f32[64,128,128]{2,1,0:T(8,128)} %all-to-all-done.tiles_ref), custom_call_target="tpu_custom_call" | custom-call | tf_op jit(solution)/shard_map/add_tiles/pallas_call | solution.py:81
  71.1 34.1 %share_lead.1 = f32[8,128,1024]{2,1,0:T(8,128)} custom-call(f32[128,1024]{1,0:T(8,128)} %get-tuple-element.14.strip_ref), custom_call_target="tpu_custom_call" | custom-call | tf_op jit(solution)/shard_map/share_lead/pallas_call | solution.py:288
  105.2 15.0 %all-to-all-start.1 = ((f32[16,128,1024]{2,1,0:T(8,128)}), f32[16,128,1024]{2,1,0:T(8,128)}, u32[]{:S(2)}, u32[]{:S(2)}) async-start(f32[16,128,1024]{2,1,0:T(8,128)} %get-tuple-element.15), calls=%async_computation.1 | async-start | bytes 16777216 | tf_op jit(solution)/shard_map/all_to_all | solution.py:685
  120.2 58.4 %factor.1 = (f32[128,1024]{1,0:T(8,128)}, f32[128,1024]{1,0:T(8,128)}) custom-call(f32[1024,1024]{1,0:T(8,128)} %bitcast.5, f32[128,1024]{1,0:T(8,128)} %get-tuple-element.14.strip_ref), custom_call_target="tpu_custom_call" | custom-call | tf_op jit(solution)/shard_map/factor/pallas_call | solution.py:459
  178.7 90.7 %share_solved.1 = (f32[16,128,1024]{2,1,0:T(8,128)}, f32[8,128,1024]{2,1,0:T(8,128)}) custom-call(f32[128,1024]{1,0:T(8,128)} %get-tuple-element.17.mine_ref), custom_call_target="tpu_custom_call" | custom-call | tf_op jit(solution)/shard_map/share_solved/pallas_call | solution.py:609
  269.4 0.0 all-to-all-done.1
  269.4 19.8 %update.1 = f32[2048,1024]{1,0:T(8,128)} custom-call(f32[2048,1024]{1,0:T(8,128)} %bitcast.1.front_ref, f32[2048,1024]{1,0:T(8,128)} %bitcast.6, f32[1024,1024]{1,0:T(8,128)} %bitcast.7, f32[128,1024]{1,0:T(8,128)} %get-tuple-element.20.shown_ref), custom_call_target="tpu_custom_call" | custom-call | tf_op jit(solution)/shard_map/update/pallas_call | solution.py:661
  (1 shorter events, 0.0 us)
Async XLA Ops:
  0.0 7.6 %copy-start = (s32[64,2]{0,1:T(2,128)S(1)}, s32[64,2]{0,1:T(2,128)}, u32[]{:S(2)}) copy-start(s32[64,2]{0,1:T(2,128)} %param.5) | copy-start | bytes 1540
  0.0 60.0 %all-to-all-start = ((f32[64,128,128]{2,1,0:T(8,128)}), f32[64,128,128]{2,1,0:T(8,128)}, u32[]{:S(2)}, u32[]{:S(2)}) async-start(f32[64,128,128]{2,1,0:T(8,128)} %param.4), calls=%async_computation | async-start | bytes 8388608 | tf_op jit(solution)/shard_map/all_to_all | solution.py:681
  105.2 164.2 %all-to-all-start.1 = ((f32[16,128,1024]{2,1,0:T(8,128)}), f32[16,128,1024]{2,1,0:T(8,128)}, u32[]{:S(2)}, u32[]{:S(2)}) async-start(f32[16,128,1024]{2,1,0:T(8,128)} %get-tuple-element.15), calls=%async_computation.1 | async-start | bytes 16777216 | tf_op jit(solution)/shard_map/all_to_all | solution.py:685
